TPU v7x, 512 devices: a whole 4x4x16 slice. The times are simulated.
512 devices in a mesh: sec: 16 (over z_lo, y), tile: 32 (over x, z_hi, core).
Axes of the slice: x: 4, y: 4, z: 16 (z_hi: 4, z_lo: 4; z = z_hi * 4 + z_lo), core: 2. Of those that a mesh axis runs over, the one named last changes fastest.
Arguments:
- snapshots: bfloat16 [5, 256, 3072, 256], P(None, 'sec', 'tile'), may hold values from -6 to 6
- eig_columns: bfloat16 [256, 256], P(None, 'tile'), may hold values from -0.375 to 0.375
- mean_u: float32 [256, 3072], P('sec', 'tile'), may hold values from 0.2 to 1
- mean_v: float32 [256, 3072], P('sec', 'tile'), may hold values from -0.5 to 0.5
- mean_rho: float32 [256, 3072], P('sec', 'tile'), may hold values from 0.5 to 2
- mean_shear: float32 [256, 3072], P('sec', 'tile'), may hold values from 0.2 to 2
- sound: float32 [256, 3072], P('sec', 'tile'), may hold values from 0.5 to 4
Outputs:
- rayleigh: float32 [16, 256, 256], P('sec', 'tile')
All inputs are finite; a program needn't handle non-finite values.
Results may differ from a plain program's by a relative error of at most 0.0044.
Values may be sent and summed in bfloat16 or wider, within the bound.
No kernel may reach another device: no remote copies, remote signals or barrier semaphores. Data moves between devices by JAX's collectives and lax.ppermute only.
A program may use at most 64 MiB of HBM per device.

v0:
```python
import jax
import jax.numpy as jnp
from jax import lax
from jax.sharding import PartitionSpec as P

viscosity = 0.002


def extended(cells, sides, width):
    for axis, dim in sides:
        count = lax.axis_size(axis)
        ends = count - 1
        head = lax.slice_in_dim(cells, 0, width, axis=dim)
        tail = lax.slice_in_dim(cells, cells.shape[dim] - width, cells.shape[dim], axis=dim)
        cells = jnp.concatenate(
            [
                lax.ppermute(tail, axis, [(i, (i + 1) % count) for i in range(ends)]),
                cells,
                lax.ppermute(head, axis, [((i + 1) % count, i) for i in range(ends)]),
            ],
            axis=dim,
        )
    return cells


def prefix(value, axis, join, neutral):
    count, mine = (lax.axis_size(axis), lax.axis_index(axis))
    pieces = lax.all_gather(value, axis)
    subtotal = jnp.full_like(value, 0) + jnp.asarray(neutral, value.dtype)

    def lap(position, subtotal):
        longer = join(subtotal, pieces[position])
        return jnp.where(position < mine, longer, subtotal)

    return lax.fori_loop(0, count - 1, lap, subtotal)


def field_at(padded, k, off_x, off_y):
    end_x = padded.shape[1] - 1 + off_x
    end_y = padded.shape[2] - 1 + off_y
    return padded[k, 1 + off_x : end_x, 1 + off_y : end_y, :].astype(jnp.float32)


def gradient(padded, k):
    along_x = (field_at(padded, k, 1, 0) - field_at(padded, k, -1, 0)) * 0.5
    along_y = (field_at(padded, k, 0, 1) - field_at(padded, k, 0, -1)) * 0.5
    return (along_x, along_y)


def laplace(padded, k):
    total = field_at(padded, k, 1, 0) + field_at(padded, k, -1, 0)
    total = total + field_at(padded, k, 0, 1) + field_at(padded, k, 0, -1)
    return total - 4.0 * field_at(padded, k, 0, 0)


def stencil(padded, mean_u, mean_v, mean_rho, mean_shear, sound):
    flow_x = mean_u[:, :, None]
    flow_y = mean_v[:, :, None]
    density = mean_rho[:, :, None]
    inverse = 1.0 / density
    shear = mean_shear[:, :, None]
    stiff = sound[:, :, None]
    rho_x, rho_y = gradient(padded, 0)
    u_x, u_y = gradient(padded, 1)
    v_x, v_y = gradient(padded, 2)
    w_x, w_y = gradient(padded, 3)
    p_x, p_y = gradient(padded, 4)
    diverge = u_x + v_y
    image_rho = -(flow_x * rho_x + flow_y * rho_y) - density * diverge
    image_u = (
        -(flow_x * u_x + flow_y * u_y)
        - shear * field_at(padded, 2, 0, 0)
        - inverse * p_x
        + viscosity * laplace(padded, 1)
    )
    image_v = -(flow_x * v_x + flow_y * v_y) - inverse * p_y + viscosity * laplace(padded, 2)
    image_w = -(flow_x * w_x + flow_y * w_y) + viscosity * laplace(padded, 3)
    image_p = -(flow_x * p_x + flow_y * p_y) - stiff * diverge
    return jnp.stack([image_rho, image_u, image_v, image_w, image_p]).astype(jnp.bfloat16)


def form_modes(block, piece):
    return jnp.einsum("fxys,sk->fxyk", block, piece, preferred_element_type=jnp.float32).astype(
        jnp.bfloat16
    )


def add_blocks(earlier, later):
    return earlier + later


def body(snapshots, eig_columns, mean_u, mean_v, mean_rho, mean_shear, sound):
    sections = lax.axis_size("sec")
    tiles_n = lax.axis_size("tile")
    cells_x = snapshots.shape[1]
    cells_y = snapshots.shape[2]
    scale = float(5 * cells_x * cells_y * sections * tiles_n) ** (-0.5)
    modes = form_modes(snapshots, lax.all_gather(eig_columns, "tile", axis=1, tiled=True))
    padded = extended(modes, (("sec", 1), ("tile", 2)), 1)
    image = stencil(padded, mean_u, mean_v, mean_rho, mean_shear, sound)
    own_rows = lax.psum_scatter(
        jnp.einsum("fxyk,fxyl->kl", modes, image, preferred_element_type=jnp.float32) * scale,
        "tile",
        scatter_dimension=0,
        tiled=True,
    )
    upstream = prefix(own_rows, "sec", add_blocks, jnp.zeros_like(own_rows))
    prefix_sum = upstream + own_rows
    return prefix_sum[None]


def solution(mesh):
    in_specs = (
        P(None, "sec", "tile", None),
        P(None, "tile"),
        P("sec", "tile"),
        P("sec", "tile"),
        P("sec", "tile"),
        P("sec", "tile"),
        P("sec", "tile"),
    )
    out_specs = P("sec", "tile", None)
    return jax.shard_map(body, mesh=mesh, in_specs=in_specs, out_specs=out_specs, check_vma=False)
```

profile of v0, /device:TPU:2, one launch (start us, length us, event | category | flops | bytes accessed | tf_op | source)
XLA Modules:
  0.0 275.3 jit_solution(12448692880432046577)
XLA Ops:
  6.5 0.0 reduce-scatter.2.cloned.1.call-start
  6.5 55.4 %all_gather.9 = bf16[256,256]{0,1:T(8,128)(2,1)S(1)} all-gather(bf16[256,8]{0,1:T(8,128)(2,1)} %param.10), channel_id=1, replica_groups=mesh['sec'=16,'tile'=32] {'tile'}, dimensions={1}, use_global_device_ids=true | all-gather | bytes 135168 | tf_op jit(solution)/shard_map/all_gather | solution.py:98
  61.9 0.0 copy-start.1
  61.9 0.0 copy-start.2
  61.9 3.4 %convolution_convert_fusion = bf16[5,16,96,256]{3,2,1,0:T(8,128)(2,1)S(1)} fusion(bf16[5,16,96,256]{3,2,1,0:T(8,128)(2,1)} %param.9, bf16[256,256]{0,1:T(8,128)(2,1)S(1)} %all_gather.9), kind=kOutput, calls=%fused_computation.1 | convolution fusion | flops 1008599040 | bytes 7995392 | tf_op jit(solution)/shard_map/fxys,sk->fxyk/dot_general | solution.py:83
  65.3 1.3 collective-permute-start
  66.6 4.6 %collective-permute-start.1 = (bf16[5,1,96,256]{3,2,1,0:T(8,128)(2,1)S(1)}, bf16[5,1,96,256]{3,2,1,0:T(8,128)(2,1)S(1)}, u32[]{:S(2)}, u32[]{:S(2)}) collective-permute-start(bf16[5,1,96,256]{3,2,1,0:T(8,128)(2,1)S(1)} %get-tuple-element.110), channel_id=1, source_target_pairs={{0,32},{32,64},{64,96},{96,128},{128,160},{160,192},{192,224},{224... | collective-permute-start | bytes 737288 | tf_op jit(solution)/shard_map/ppermute | solution.py:17
  71.2 0.0 copy-done.1
  71.2 0.0 copy-done.2
  71.2 0.0 copy-start.3
  71.2 0.0 copy-start.4
  71.2 4.2 %collective-permute-done = bf16[5,1,96,256]{3,2,1,0:T(8,128)(2,1)S(1)} collective-permute-done((bf16[5,1,96,256]{3,2,1,0:T(8,128)(2,1)S(1)}, bf16[5,1,96,256]{3,2,1,0:T(8,128)(2,1)S(1)}, u32[]{:S(2)}, u32[]{:S(2)}) %collective-permute-start) | collective-permute-done | bytes 245792 | tf_op jit(solution)/shard_map/ppermute | solution.py:19
  75.4 1.2 collective-permute-done.1
  76.6 0.1 pad_maximum_fusion.18
  76.7 4.2 %collective-permute-start.2 = (bf16[5,18,1,256]{3,2,1,0:T(2,128)(2,1)S(1)}, bf16[5,18,1,256]{3,2,1,0:T(2,128)(2,1)S(1)}, u32[]{:S(2)}, u32[]{:S(2)}) collective-permute-start(bf16[5,18,1,256]{3,2,1,0:T(2,128)(2,1)S(1)} %get-tuple-element.108), channel_id=1, source_target_pairs={{1,0},{2,1},{3,2},{4,3},{5,4},{6,5},{7,6},{8,7},{9,8},{10,9},{11,1... | collective-permute-start | bytes 138248 | tf_op jit(solution)/shard_map/ppermute | solution.py:19
  80.9 1.9 collective-permute-start.3
  82.9 0.0 copy-done.3
  82.9 0.0 copy-done.4
  82.9 0.2 collective-permute-done.2
  83.1 8.5 %collective-permute-done.3 = bf16[5,18,1,256]{3,2,1,0:T(2,128)(2,1)S(1)} collective-permute-done((bf16[5,18,1,256]{3,2,1,0:T(2,128)(2,1)S(1)}, bf16[5,18,1,256]{3,2,1,0:T(2,128)(2,1)S(1)}, u32[]{:S(2)}, u32[]{:S(2)}) %collective-permute-start.3) | collective-permute-done | bytes 46112 | tf_op jit(solution)/shard_map/ppermute | solution.py:17
  91.6 0.0 copy-start
  91.6 5.0 %fusion.27 = bf16[5,16,96,256]{3,2,1,0:T(8,128)(2,1)S(1)} fusion(bf16[5,18,1,256]{3,2,1,0:T(2,128)(2,1)S(1)} %collective-permute-done.3, bf16[5,1,96,256]{3,2,1,0:T(8,128)(2,1)S(1)} %collective-permute-done, bf16[5,16,96,256]{3,2,1,0:T(8,128)(2,1)S(1)} %convolution_convert_fusion, bf16[5,1,96,256]{3,2,1,0:T(8,128)(2,1)S(1)} %collective-permute-done.1, ...), kind=kLoop, calls=%fused_computation.51 | loop fusion | flops 23592960 | bytes 5320704
  96.6 0.0 copy-done
  96.6 2.6 fusion.30
  99.2 5.2 %fusion.31 = bf16[5,16,96,256]{3,2,1,0:T(8,128)(2,1)S(1)} fusion(bf16[5,16,96,256]{3,2,1,0:T(8,128)(2,1)S(1)} %fusion.30, bf16[5,16,96,256]{3,2,1,0:T(8,128)(2,1)S(1)} %convolution_convert_fusion, bf16[5,1,96,256]{3,2,1,0:T(8,128)(2,1)S(1)} %collective-permute-done.1, bf16[5,1,96,256]{3,2,1,0:T(8,128)(2,1)S(1)} %collective-permute-done, ...), kind=kLoop, calls=%fused_computation.55 | loop fusion | flops 22806528 | bytes 6205440
  104.5 2.1 fusion.29
  106.6 5.7 %fusion.28 = bf16[5,16,96,256]{3,2,1,0:T(8,128)(2,1)S(1)} fusion(bf16[5,16,96,256]{3,2,1,0:T(8,128)(2,1)S(1)} %fusion.29, f32[16,96]{1,0:T(8,128)S(1)} %get-tuple-element.115, f32[16,96]{1,0:T(8,128)S(1)} %get-tuple-element.114, f32[16,96]{1,0:T(8,128)S(1)} %get-tuple-element.116, bf16[5,1,96,256]{3,2,1,0:T(8,128)(2,1)S(1)} %collective-permute-done, ...), kind=kLoop, calls=%fused_computation.52 | loop fusion | flops 23592960 | bytes 5419008 | tf_op jit(solution)/shard_map/stack | solution.py:79
  112.3 1.9 fusion.26
  114.2 0.0 reduce-scatter.2.cloned.1.call-update
  114.3 110.3 %reduce-scatter.2.cloned.1.call-done = f32[8,256]{1,0:T(8,128)} async-done(((f32[256,256]{1,0:T(8,128)}), f32[8,256]{1,0:T(8,128)}) %reduce-scatter.2.cloned.1.call-update) | async-done | bytes 8208 | tf_op jit(solution)/shard_map/reduce_scatter | solution.py:101
  224.6 42.1 %all-gather = f32[128,256]{1,0:T(8,128)S(1)} all-gather(f32[8,256]{1,0:T(8,128)} %reduce-scatter.2.cloned.1.call-done), channel_id=2, replica_groups=mesh['sec'=16,'tile'=32] {'sec'}, dimensions={0}, use_global_device_ids=true | all-gather | bytes 139264 | tf_op jit(solution)/shard_map/all_gather | solution.py:28
  266.7 0.5 while.14
  267.2 1.3 add_bitcast_fusion
  (19 shorter events, 0.2 us)
Async XLA Ops:
  6.5 218.1 %reduce-scatter.2.cloned.1.call-start = ((), (), s32[]{:S(2)}) async-start(), calls=%async_computation.1 | async-start | bytes 270336 | tf_op jit(solution)/shard_map/reduce_scatter | solution.py:101
  61.9 9.3 %copy-start.1 = (f32[16,96]{1,0:T(8,128)S(1)}, f32[16,96]{1,0:T(8,128)}, u32[]{:S(2)}) copy-start(f32[16,96]{1,0:T(8,128)} %param.13) | copy-start | bytes 18436
  61.9 9.3 %copy-start.2 = (f32[16,96]{1,0:T(8,128)S(1)}, f32[16,96]{1,0:T(8,128)}, u32[]{:S(2)}) copy-start(f32[16,96]{1,0:T(8,128)} %param.12) | copy-start | bytes 18436
  65.3 10.1 %collective-permute-start = (bf16[5,1,96,256]{3,2,1,0:T(8,128)(2,1)S(1)}, bf16[5,1,96,256]{3,2,1,0:T(8,128)(2,1)S(1)}, u32[]{:S(2)}, u32[]{:S(2)}) collective-permute-start(bf16[5,1,96,256]{3,2,1,0:T(8,128)(2,1)S(1)} %get-tuple-element.111), channel_id=1, source_target_pairs={{32,0},{64,32},{96,64},{128,96},{160,128},{192,160},{224,192},{256... | collective-permute-start | bytes 737288 | tf_op jit(solution)/shard_map/ppermute | solution.py:19
  66.6 10.0 %collective-permute-start.1 = (bf16[5,1,96,256]{3,2,1,0:T(8,128)(2,1)S(1)}, bf16[5,1,96,256]{3,2,1,0:T(8,128)(2,1)S(1)}, u32[]{:S(2)}, u32[]{:S(2)}) collective-permute-start(bf16[5,1,96,256]{3,2,1,0:T(8,128)(2,1)S(1)} %get-tuple-element.110), channel_id=1, source_target_pairs={{0,32},{32,64},{64,96},{96,128},{128,160},{160,192},{192,224},{224... | collective-permute-start | bytes 737288 | tf_op jit(solution)/shard_map/ppermute | solution.py:17
  71.2 11.7 %copy-start.3 = (f32[16,96]{1,0:T(8,128)S(1)}, f32[16,96]{1,0:T(8,128)}, u32[]{:S(2)}) copy-start(f32[16,96]{1,0:T(8,128)} %param.15) | copy-start | bytes 18436
  71.2 11.7 %copy-start.4 = (f32[16,96]{1,0:T(8,128)S(1)}, f32[16,96]{1,0:T(8,128)}, u32[]{:S(2)}) copy-start(f32[16,96]{1,0:T(8,128)} %param.11) | copy-start | bytes 18436
  76.7 6.3 %collective-permute-start.2 = (bf16[5,18,1,256]{3,2,1,0:T(2,128)(2,1)S(1)}, bf16[5,18,1,256]{3,2,1,0:T(2,128)(2,1)S(1)}, u32[]{:S(2)}, u32[]{:S(2)}) collective-permute-start(bf16[5,18,1,256]{3,2,1,0:T(2,128)(2,1)S(1)} %get-tuple-element.108), channel_id=1, source_target_pairs={{1,0},{2,1},{3,2},{4,3},{5,4},{6,5},{7,6},{8,7},{9,8},{10,9},{11,1... | collective-permute-start | bytes 138248 | tf_op jit(solution)/shard_map/ppermute | solution.py:19
  80.9 10.7 %collective-permute-start.3 = (bf16[5,18,1,256]{3,2,1,0:T(2,128)(2,1)S(1)}, bf16[5,18,1,256]{3,2,1,0:T(2,128)(2,1)S(1)}, u32[]{:S(2)}, u32[]{:S(2)}) collective-permute-start(bf16[5,18,1,256]{3,2,1,0:T(2,128)(2,1)S(1)} %get-tuple-element.109), channel_id=1, source_target_pairs={{0,1},{1,2},{2,3},{3,4},{4,5},{5,6},{6,7},{7,8},{8,9},{9,10},{10,1... | collective-permute-start | bytes 138248 | tf_op jit(solution)/shard_map/ppermute | solution.py:17
  91.6 5.0 %copy-start = (f32[16,96]{1,0:T(8,128)S(1)}, f32[16,96]{1,0:T(8,128)}, u32[]{:S(2)}) copy-start(f32[16,96]{1,0:T(8,128)} %param.14) | copy-start | bytes 18436
Sparse Core Ops, SparseCore 0:
  114.4 110.1 reduce-scatter.1
where the time goes:
time: 276 us; the launch traced here: 275 us
  waiting for transfers between devices  124 us (45%)
  blocking collectives  97.4 us (35%)
  other arithmetic  22.2 us (8%)
  between operations  13.6 us (5%)
  starting transfers between devices  12 us (4%)
  matrix products  5.3 us (2%)
    reduce_scatter x1, waiting for transfers between devices, body(): lax.psum_scatter(jnp.einsum('fxyk,fxyl->kl', modes, image, preferred_elem...  110 us
    all_gather x1, blocking collectives, body(): lax.all_gather(eig_columns, 'tile', axis=1, tiled=True)  55.4 us
    all_gather x1, blocking collectives, prefix(): pieces = lax.all_gather(value, axis)  42.1 us
    unnamed x5, other arithmetic  14.9 us
    ppermute x2, waiting for transfers between devices, extended(): lax.ppermute(tail, axis, [(i, (i + 1) % count) for i in range(ends)])  9.72 us
    ppermute x2, starting transfers between devices, extended(): lax.ppermute(tail, axis, [(i, (i + 1) % count) for i in range(ends)])  6.48 us
    another operation x1, other arithmetic, stencil(): jnp.stack([image_rho, image_u, image_v, image_w, image_p])  5.68 us
  transfers between devices with their start and end apart: 5, of which 5 were waited for; matrix products, arithmetic and copies ran while one was open for 0% of the time, Pallas kernels for 0%

commit v1 on v0

v1 whole, which is shorter than its diff:
```python
import jax
import jax.numpy as jnp
from jax import lax
from jax.experimental import pallas as pl
from jax.experimental.pallas import tpu as pltpu
from jax.sharding import PartitionSpec as P

viscosity = 0.002
pad = 8
strip = 16


def interior_kernel(x_hbm, mu, mv, mr, ms, mc, g_ref, ct_ref, xb, qf, raw, image, sems):
    fields, nx, ny, modes = x_hbm.shape

    def copy(i):
        return pltpu.make_async_copy(x_hbm.at[:, i], xb.at[i], sems.at[i])

    for i in range(nx):
        copy(i).start()

    raw[...] = jnp.zeros_like(raw)
    for j, value in enumerate(
        (mu[...] * -0.5, mv[...] * -0.5, mr[...] * -0.5, -ms[...], -0.5 / mr[...], mc[...] * -0.5)
    ):
        raw[j * nx : (j + 1) * nx, 0:ny] = value
    ct_ref[...] = raw[...].T
    qf[0] = jnp.zeros(qf.shape[1:], jnp.float32)
    qf[nx + 1] = jnp.zeros(qf.shape[1:], jnp.float32)
    g_ref[...] = jnp.zeros_like(g_ref)

    def widen(i):
        copy(i).wait()
        edge = jnp.zeros((pad, modes), jnp.float32)
        for f in range(fields):
            qf[i + 1, f, 0:pad] = edge
            qf[i + 1, f, pad + ny : 2 * pad + ny] = edge
            for y in range(0, ny, strip):
                qf[i + 1, f, pad + y : pad + y + strip] = xb[i, f, y : y + strip].astype(jnp.float32)

    def apply(i):
        turned = pltpu.roll(ct_ref[...], 128 - i, 1)
        for y in range(0, ny, strip):
            column = turned[y : y + strip]
            half_u, half_v, half_rho, shear, half_inverse, half_sound = (
                jnp.broadcast_to(column[:, j * nx : j * nx + 1], (strip, modes)) for j in range(6)
            )
            east_c, west_c = viscosity + half_u, viscosity - half_u
            north_c, south_c = viscosity + half_v, viscosity - half_v
            top = pad + y

            def east(f):
                return qf[i + 2, f, top : top + strip]

            def west(f):
                return qf[i, f, top : top + strip]

            def north(f):
                return qf[i + 1, f, top + 1 : top + 1 + strip]

            def south(f):
                return qf[i + 1, f, top - 1 : top - 1 + strip]

            def here(f):
                return qf[i + 1, f, top : top + strip]

            def flow(f):
                return half_u * (east(f) - west(f)) + half_v * (north(f) - south(f))

            def spread(f):
                return (
                    east_c * east(f) + west_c * west(f) + north_c * north(f) + south_c * south(f)
                ) - (4.0 * viscosity) * here(f)

            diverge = (east(1) - west(1)) + (north(2) - south(2))
            images = (
                flow(0) + half_rho * diverge,
                spread(1) + shear * here(2) + half_inverse * (east(4) - west(4)),
                spread(2) + half_inverse * (north(4) - south(4)),
                spread(3),
                flow(4) + half_sound * diverge,
            )
            for f in range(fields):
                high = images[f].astype(jnp.bfloat16)
                low = (images[f] - high.astype(jnp.float32)).astype(jnp.bfloat16)
                image[f * ny + y : f * ny + y + strip, 0:modes] = high
                image[f * ny + y : f * ny + y + strip, modes : 2 * modes] = low
        g_ref[...] += lax.dot_general(
            xb[i].reshape(fields * ny, modes),
            image[...],
            (((0,), (0,)), ((), ())),
            preferred_element_type=jnp.float32,
        )

    widen(0)

    def step(i, carry):
        @pl.when(i + 1 < nx)
        def _():
            widen(i + 1)

        apply(i)
        return carry

    lax.fori_loop(0, nx, step, 0)


def interior(snapshots, *means):
    fields, nx, ny, modes = snapshots.shape
    return pl.pallas_call(
        interior_kernel,
        out_shape=(
            jax.ShapeDtypeStruct((modes, 2 * modes), jnp.float32),
            jax.ShapeDtypeStruct((128, 128), jnp.float32),
        ),
        in_specs=[pl.BlockSpec(memory_space=pltpu.HBM)] + [pl.BlockSpec(memory_space=pltpu.VMEM)] * 5,
        out_specs=(pl.BlockSpec(memory_space=pltpu.VMEM),) * 2,
        scratch_shapes=[
            pltpu.VMEM((nx, fields, ny, modes), jnp.bfloat16),
            pltpu.VMEM((nx + 2, fields, ny + 2 * pad, modes), jnp.float32),
            pltpu.VMEM((128, 128), jnp.float32),
            pltpu.VMEM((fields * ny, 2 * modes), jnp.bfloat16),
            pltpu.SemaphoreType.DMA((nx,)),
        ],
        compiler_params=pltpu.CompilerParams(vmem_limit_bytes=20 << 20),
        cost_estimate=pl.CostEstimate(flops=20 * 10**9, transcendentals=0, bytes_accessed=10**7),
        name="interior",
    )(snapshots, *means)


def split(value):
    high = value.astype(jnp.bfloat16)
    rest = value - high.astype(jnp.float32)
    middle = rest.astype(jnp.bfloat16)
    return high, middle, (rest - middle.astype(jnp.float32)).astype(jnp.bfloat16)


def contract(left, right):
    return lax.dot_general(left, right, (((0,), (0,)), ((), ())), preferred_element_type=jnp.float32)


def finish_kernel(
    scale, g_ref, ct_ref, head_x, tail_x, from_west, from_east, tail_y, from_north,
    mv, mr, mc, vt_ref, out_ref
):
    modes = g_ref.shape[0]
    ny = head_x.shape[2]
    nx = tail_y.shape[1]
    total = g_ref[:, 0:modes] + g_ref[:, modes : 2 * modes]

    def side(own, other, column, along, cross, sign):
        half_c, half_rho, half_inverse, half_sound = (sign * c for c in column)
        spread_c = viscosity + half_c
        images = [
            half_c * other(0) + half_rho * other(along),
            spread_c * other(1),
            spread_c * other(2),
            spread_c * other(3),
            half_c * other(4) + half_sound * other(along),
        ]
        images[along] = images[along] + half_inverse * other(4)
        added = None
        for f in range(5):
            high, middle, _ = split(images[f])
            one = contract(own(f), high) + contract(own(f), middle)
            added = one if added is None else added + one
        return added

    def plane(ref):
        return lambda f: ref[f, 0].astype(jnp.float32)

    def column_x(i):
        return tuple(ct_ref[0:ny, j * nx + i : j * nx + i + 1] for j in (0, 2, 4, 5))

    total += side(lambda f: head_x[f, 0], plane(from_west), column_x(0), 1, 2, -1.0)
    total += side(lambda f: tail_x[f, 0], plane(from_east), column_x(nx - 1), 1, 2, 1.0)

    own_column = tuple(
        c for c in (mv[:, ny - 1 : ny] * -0.5, mr[:, ny - 1 : ny] * -0.5, -0.5 / mr[:, ny - 1 : ny], mc[:, ny - 1 : ny] * -0.5)
    )
    packed = from_north[5].astype(jnp.float32)
    other_column = tuple(
        packed[:, 3 * j : 3 * j + 1] + packed[:, 3 * j + 1 : 3 * j + 2] + packed[:, 3 * j + 2 : 3 * j + 3]
        for j in range(4)
    )
    wide = lambda ref: (lambda f: ref[f].astype(jnp.float32))
    total += side(lambda f: tail_y[f], wide(from_north), own_column, 2, 1, 1.0)
    total += side(lambda f: from_north[f], wide(tail_y), other_column, 2, 1, -1.0)

    vt = vt_ref[...]
    right = None
    for part in split(total):
        one = lax.dot_general(part, vt, (((1,), (1,)), ((), ())), preferred_element_type=jnp.float32)
        right = one if right is None else right + one
    both = None
    for part in split(right):
        one = jnp.dot(vt, part, preferred_element_type=jnp.float32)
        both = one if both is None else both + one
    out_ref[...] = (both * scale).astype(out_ref.dtype)


def finish(scale, *operands):
    import functools

    modes = operands[-1].shape[0]
    return pl.pallas_call(
        functools.partial(finish_kernel, scale),
        out_shape=jax.ShapeDtypeStruct((modes, modes), jnp.float32),
        in_specs=[pl.BlockSpec(memory_space=pltpu.VMEM)] * len(operands),
        out_specs=pl.BlockSpec(memory_space=pltpu.VMEM),
        compiler_params=pltpu.CompilerParams(vmem_limit_bytes=12 << 20),
        name="finish",
    )(*operands)


def pieces(value):
    high = lax.reduce_precision(value, 8, 7)
    rest = value - high
    middle = lax.reduce_precision(rest, 8, 7)
    return [high, middle, rest - middle]


def body(snapshots, eig_columns, mean_u, mean_v, mean_rho, mean_shear, sound):
    sections = lax.axis_size("sec")
    tiles_n = lax.axis_size("tile")
    fields, nx, ny, modes = snapshots.shape
    rows = modes // tiles_n
    scale = float(fields * nx * ny * sections * tiles_n) ** (-0.5)

    first = (mean_v[:, 0], mean_rho[:, 0], sound[:, 0])
    sent = [first[0] * -0.5, first[1] * -0.5, -0.5 / first[1], first[2] * -0.5]
    packed = jnp.stack([p for value in sent for p in pieces(value)], axis=-1)
    packed = jnp.pad(packed, ((0, 0), (0, modes - packed.shape[1])))
    head_y = jnp.concatenate([snapshots[:, :, 0], packed[None].astype(jnp.bfloat16)])
    tail_y = snapshots[:, :, ny - 1]
    from_north = lax.ppermute(head_y, "tile", [(i + 1, i) for i in range(tiles_n - 1)])
    own = jnp.broadcast_to(eig_columns.T[None], (tiles_n, rows, modes))
    vt = lax.all_to_all(own, "tile", 0, 0, tiled=True).reshape(modes, modes)
    head_x = snapshots[:, :1]
    tail_x = snapshots[:, nx - 1 :]
    from_west = lax.ppermute(tail_x, "sec", [(i, i + 1) for i in range(sections - 1)])
    from_east = lax.ppermute(head_x, "sec", [(i + 1, i) for i in range(sections - 1)])

    gram, columns = interior(snapshots, mean_u, mean_v, mean_rho, mean_shear, sound)
    local = finish(
        scale, gram, columns, head_x, tail_x, from_west, from_east, tail_y, from_north,
        mean_v, mean_rho, sound, vt
    )
    shares = lax.all_to_all(local.reshape(tiles_n, rows, modes), "tile", 0, 0, tiled=True)
    term = shares.sum(0)
    terms = lax.all_to_all(
        jnp.broadcast_to(term[None], (sections, rows, modes)), "sec", 0, 0, tiled=True
    )
    upstream = jnp.arange(sections) <= lax.axis_index("sec")
    return jnp.where(upstream[:, None, None], terms, 0.0).sum(0)[None]


def solution(mesh):
    in_specs = (
        P(None, "sec", "tile", None),
        P(None, "tile"),
        P("sec", "tile"),
        P("sec", "tile"),
        P("sec", "tile"),
        P("sec", "tile"),
        P("sec", "tile"),
    )
    out_specs = P("sec", "tile", None)
    return jax.shard_map(body, mesh=mesh, in_specs=in_specs, out_specs=out_specs, check_vma=False)
```

time: 276 us -> 107 us (0.39)
  the two profiles are of different devices: /device:TPU:2 before, /device:TPU:1 now
where the time goes in v1:
time: 107 us; the launch traced here: 106 us
  starting transfers between devices  36.3 us (34%)
  blocking collectives  34.6 us (32%)
  Pallas kernels  14.8 us (14%)
  local copies, waits for them, and re-layouts  10.1 us (9%)
  waiting for transfers between devices  7.78 us (7%)
  other arithmetic  2.17 us (2%)
    all_to_all x1, blocking collectives, body(): lax.all_to_all(local.reshape(tiles_n, rows, modes), 'tile', 0, 0, tiled=T...  34.6 us
    all_to_all x1, starting transfers between devices, body(): vt = lax.all_to_all(own, 'tile', 0, 0, tiled=True).reshape(modes, modes)  14.6 us
    pallas_call x1, Pallas kernels, interior(): pl.pallas_call(interior_kernel, out_shape=(jax.ShapeDtypeStruct((modes, 2...  12.2 us
    all_to_all x1, starting transfers between devices, body(): lax.all_to_all(jnp.broadcast_to(term[None], (sections, rows, modes)), 'se...  10.4 us
    ppermute x1, starting transfers between devices, body(): lax.ppermute(head_y, 'tile', [(i + 1, i) for i in range(tiles_n - 1)])  8.75 us
    all_to_all x1, waiting for transfers between devices, body(): lax.all_to_all(jnp.broadcast_to(term[None], (sections, rows, modes)), 'se...  7.77 us
    unnamed x20, local copies, waits for them, and re-layouts  5.62 us
    pallas_call x1, Pallas kernels, finish(): pl.pallas_call(functools.partial(finish_kernel, scale), out_shape=jax.Sha...  2.61 us
  transfers between devices with their start and end apart: 5, of which 1 were waited for; matrix products, arithmetic and copies ran while one was open for 2% of the time, Pallas kernels for 12%

profile of v1, /device:TPU:1, one launch (start us, length us, event | category | flops | bytes accessed | tf_op | source)
XLA Modules:
  0.0 105.9 jit_solution(6967580075300835110)
XLA Ops:
  0.0 0.7 fusion.3
  0.7 0.7 fusion
  1.4 0.1 stack.3
  1.5 1.2 %fusion.4 = (bf16[5,16,1,256]{3,2,1,0:T(2,128)(2,1)S(1)}, bf16[5,16,1,256]{3,2,1,0:T(2,128)(2,1)S(1)}) fusion(bf16[5,16,96,256]{3,2,1,0:T(8,128)(2,1)} %x_hbm.1), kind=kLoop, calls=%fused_computation.29 | loop fusion | bytes 163840 | tf_op jit(solution)/shard_map/slice | solution.py:234
  2.8 8.7 %collective-permute-start.2 = (bf16[6,16,256]{2,1,0:T(8,128)(2,1)S(1)}, bf16[6,16,256]{2,1,0:T(8,128)(2,1)S(1)}, u32[]{:S(2)}, u32[]{:S(2)}) collective-permute-start(bf16[6,16,256]{2,1,0:T(8,128)(2,1)S(1)} %pad_maximum_fusion), channel_id=1, source_target_pairs={{1,0},{2,1},{3,2},{4,3},{5,4},{6,5},{7,6},{8,7},{9,8},{10,9},{11,1... | collective-permute-start | bytes 147464 | tf_op jit(solution)/shard_map/ppermute | solution.py:236
  11.6 1.1 %fusion.5 = (bf16[5,1,96,256]{3,2,1,0:T(8,128)(2,1)S(1)}, bf16[5,1,96,256]{3,2,1,0:T(8,128)(2,1)S(1)}) fusion(bf16[5,16,96,256]{3,2,1,0:T(8,128)(2,1)} %x_hbm.1), kind=kLoop, calls=%fused_computation.30 | loop fusion | bytes 983040 | tf_op jit(solution)/shard_map/slice | solution.py:240
  12.7 1.3 %collective-permute-start = (bf16[5,1,96,256]{3,2,1,0:T(8,128)(2,1)S(1)}, bf16[5,1,96,256]{3,2,1,0:T(8,128)(2,1)S(1)}, u32[]{:S(2)}, u32[]{:S(2)}) collective-permute-start(bf16[5,1,96,256]{3,2,1,0:T(8,128)(2,1)S(1)} %get-tuple-element.11.tail_x), channel_id=1, source_target_pairs={{0,32},{32,64},{64,96},{96,128},{128,160},{160,192},{192,224},{224... | collective-permute-start | bytes 737288 | tf_op jit(solution)/shard_map/ppermute | solution.py:241
  14.0 1.3 %collective-permute-start.1 = (bf16[5,1,96,256]{3,2,1,0:T(8,128)(2,1)S(1)}, bf16[5,1,96,256]{3,2,1,0:T(8,128)(2,1)S(1)}, u32[]{:S(2)}, u32[]{:S(2)}) collective-permute-start(bf16[5,1,96,256]{3,2,1,0:T(8,128)(2,1)S(1)} %get-tuple-element.12.head_x), channel_id=1, source_target_pairs={{32,0},{64,32},{96,64},{128,96},{160,128},{192,160},{224,192},{256... | collective-permute-start | bytes 737288 | tf_op jit(solution)/shard_map/ppermute | solution.py:242
  15.3 1.4 %broadcast_in_dim.30 = bf16[32,8,256]{2,1,0:T(8,128)(2,1)} broadcast(bf16[8,256]{1,0:T(8,128)(2,1)} %bitcast.16), dimensions={1,2} | broadcast | bytes 135168 | tf_op jit(solution)/shard_map/broadcast_in_dim | solution.py:237
  16.6 14.6 %all-to-all-start = ((bf16[32,8,256]{2,1,0:T(8,128)(2,1)}), bf16[32,8,256]{2,1,0:T(8,128)(2,1)S(1)}, u32[]{:S(2)}, u32[]{:S(2)}) async-start(bf16[32,8,256]{2,1,0:T(8,128)(2,1)} %broadcast_in_dim.30), calls=%async_computation | async-start | bytes 262144 | tf_op jit(solution)/shard_map/all_to_all | solution.py:238
  31.2 0.0 copy-start
  31.2 2.1 %copy-done = bf16[5,16,96,256]{3,2,1,0:T(8,128)(2,1)S(1)} copy-done((bf16[5,16,96,256]{3,2,1,0:T(8,128)(2,1)S(1)}, bf16[5,16,96,256]{3,2,1,0:T(8,128)(2,1)}, u32[]{:S(2)}) %copy-start) | copy-done | bytes 3932184
  33.3 0.0 copy-start.1
  33.3 0.7 copy-done.1
  34.0 0.0 copy-start.3
  34.0 0.7 copy-done.3
  34.7 0.0 copy-start.5
  34.7 0.7 copy-done.5
  35.4 0.0 copy-start.7
  35.4 0.7 copy-done.7
  36.1 0.0 copy-start.8
  36.1 0.7 copy-done.8
  36.8 0.0 copy-start.2
  36.8 0.0 copy-start.4
  36.8 0.0 copy-start.6
  36.8 12.2 %interior.1 = (f32[256,512]{1,0:T(8,128)S(1)}, f32[128,128]{1,0:T(8,128)S(1)}) custom-call(bf16[5,16,96,256]{3,2,1,0:T(8,128)(2,1)S(1)} %copy-done, f32[16,96]{1,0:T(8,128)S(1)} %copy-done.7, f32[16,96]{1,0:T(8,128)S(1)} %copy-done.3, f32[16,96]{1,0:T(8,128)S(1)} %copy-done.5, f32[16,96]{1,0:T(8,128)S(1)} %copy-done.8, f32[16,96]{1,0:T(8,128)S(1)} %copy-done.1), custom_call_target="tpu_custom_call" | custom-call | flops 20000000000 | bytes 10000000 | tf_op jit(solution)/shard_map/interior/pallas_call | solution.py:110
  49.0 0.0 collective-permute-done.2.from_north
  49.1 0.0 collective-permute-done.from_west
  49.1 0.0 collective-permute-done.1.from_east
  49.1 0.0 all-to-all-done
  49.1 0.0 copy-done.2
  49.1 0.0 copy-done.4
  49.1 0.0 copy-done.6
  49.1 2.6 %finish.1 = f32[256,256]{1,0:T(8,128)S(1)} custom-call(f32[256,512]{1,0:T(8,128)S(1)} %get-tuple-element.7.g_ref, f32[128,128]{1,0:T(8,128)S(1)} %get-tuple-element.8.ct_ref, bf16[5,1,96,256]{3,2,1,0:T(8,128)(2,1)S(1)} %get-tuple-element.12.head_x, bf16[5,1,96,256]{3,2,1,0:T(8,128)(2,1)S(1)} %get-tuple-element.11.tail_x, ...), custom_call_target="tpu_custom_call" | custom-call | tf_op jit(solution)/shard_map/finish/pallas_call | solution.py:206
  51.7 34.6 %all_to_all.15 = f32[32,8,256]{2,1,0:T(8,128)S(1)} all-to-all(f32[32,8,256]{2,1,0:T(8,128)S(1)} %bitcast.12), channel_id=1, replica_groups=mesh['sec'=16,'tile'=32] {'tile'}, dimensions={0} | all-to-all | bytes 524288 | tf_op jit(solution)/shard_map/all_to_all | solution.py:249
  86.3 0.7 broadcast_in_dim.31
  87.0 10.4 %all-to-all-start.2 = ((f32[16,8,256]{2,1,0:T(8,128)}), f32[16,8,256]{2,1,0:T(8,128)S(1)}, u32[]{:S(2)}, u32[]{:S(2)}) async-start(f32[16,8,256]{2,1,0:T(8,128)} %broadcast_in_dim.31), calls=%async_computation.2 | async-start | bytes 262144 | tf_op jit(solution)/shard_map/all_to_all | solution.py:251
  97.4 7.8 %all-to-all-done.2 = f32[16,8,256]{2,1,0:T(8,128)S(1)} async-done(((f32[16,8,256]{2,1,0:T(8,128)}), f32[16,8,256]{2,1,0:T(8,128)S(1)}, u32[]{:S(2)}, u32[]{:S(2)}) %all-to-all-start.2) | async-done | bytes 131104 | tf_op jit(solution)/shard_map/all_to_all | solution.py:251
  105.2 0.7 select_reduce_fusion
  (6 shorter events, 0.1 us)
Async XLA Ops:
  2.8 46.2 %collective-permute-start.2 = (bf16[6,16,256]{2,1,0:T(8,128)(2,1)S(1)}, bf16[6,16,256]{2,1,0:T(8,128)(2,1)S(1)}, u32[]{:S(2)}, u32[]{:S(2)}) collective-permute-start(bf16[6,16,256]{2,1,0:T(8,128)(2,1)S(1)} %pad_maximum_fusion), channel_id=1, source_target_pairs={{1,0},{2,1},{3,2},{4,3},{5,4},{6,5},{7,6},{8,7},{9,8},{10,9},{11,1... | collective-permute-start | bytes 147464 | tf_op jit(solution)/shard_map/ppermute | solution.py:236
  12.7 36.4 %collective-permute-start = (bf16[5,1,96,256]{3,2,1,0:T(8,128)(2,1)S(1)}, bf16[5,1,96,256]{3,2,1,0:T(8,128)(2,1)S(1)}, u32[]{:S(2)}, u32[]{:S(2)}) collective-permute-start(bf16[5,1,96,256]{3,2,1,0:T(8,128)(2,1)S(1)} %get-tuple-element.11.tail_x), channel_id=1, source_target_pairs={{0,32},{32,64},{64,96},{96,128},{128,160},{160,192},{192,224},{224... | collective-permute-start | bytes 737288 | tf_op jit(solution)/shard_map/ppermute | solution.py:241
  14.0 35.1 %collective-permute-start.1 = (bf16[5,1,96,256]{3,2,1,0:T(8,128)(2,1)S(1)}, bf16[5,1,96,256]{3,2,1,0:T(8,128)(2,1)S(1)}, u32[]{:S(2)}, u32[]{:S(2)}) collective-permute-start(bf16[5,1,96,256]{3,2,1,0:T(8,128)(2,1)S(1)} %get-tuple-element.12.head_x), channel_id=1, source_target_pairs={{32,0},{64,32},{96,64},{128,96},{160,128},{192,160},{224,192},{256... | collective-permute-start | bytes 737288 | tf_op jit(solution)/shard_map/ppermute | solution.py:242
  16.6 32.4 %all-to-all-start = ((bf16[32,8,256]{2,1,0:T(8,128)(2,1)}), bf16[32,8,256]{2,1,0:T(8,128)(2,1)S(1)}, u32[]{:S(2)}, u32[]{:S(2)}) async-start(bf16[32,8,256]{2,1,0:T(8,128)(2,1)} %broadcast_in_dim.30), calls=%async_computation | async-start | bytes 262144 | tf_op jit(solution)/shard_map/all_to_all | solution.py:238
  31.2 2.1 %copy-start = (bf16[5,16,96,256]{3,2,1,0:T(8,128)(2,1)S(1)}, bf16[5,16,96,256]{3,2,1,0:T(8,128)(2,1)}, u32[]{:S(2)}) copy-start(bf16[5,16,96,256]{3,2,1,0:T(8,128)(2,1)} %x_hbm.1) | copy-start | bytes 11796484
  33.3 0.7 copy-start.1
  34.0 0.7 copy-start.3
  34.7 0.7 copy-start.5
  35.4 0.7 copy-start.7
  36.1 0.7 copy-start.8
  36.8 12.3 %copy-start.2 = (f32[16,96]{1,0:T(8,128)S(1)}, f32[16,96]{1,0:T(8,128)}, u32[]{:S(2)}) copy-start(f32[16,96]{1,0:T(8,128)} %mc.3) | copy-start | bytes 18436
  36.8 12.3 %copy-start.4 = (f32[16,96]{1,0:T(8,128)S(1)}, f32[16,96]{1,0:T(8,128)}, u32[]{:S(2)}) copy-start(f32[16,96]{1,0:T(8,128)} %mv.3) | copy-start | bytes 18436
  36.8 12.3 %copy-start.6 = (f32[16,96]{1,0:T(8,128)S(1)}, f32[16,96]{1,0:T(8,128)}, u32[]{:S(2)}) copy-start(f32[16,96]{1,0:T(8,128)} %mr.3) | copy-start | bytes 18436
  87.0 18.2 %all-to-all-start.2 = ((f32[16,8,256]{2,1,0:T(8,128)}), f32[16,8,256]{2,1,0:T(8,128)S(1)}, u32[]{:S(2)}, u32[]{:S(2)}) async-start(f32[16,8,256]{2,1,0:T(8,128)} %broadcast_in_dim.31), calls=%async_computation.2 | async-start | bytes 262144 | tf_op jit(solution)/shard_map/all_to_all | solution.py:251

commit v2 on v1

--- a/solution.py
+++ b/solution.py
@@ -1,3 +1,5 @@
+import functools
+
 import jax
 import jax.numpy as jnp
 from jax import lax
@@ -10,19 +12,26 @@
 strip = 16
 
 
-def interior_kernel(x_hbm, mu, mv, mr, ms, mc, g_ref, ct_ref, xb, qf, raw, image, sems):
+def interior_kernel(x_hbm, mu_hbm, mv_hbm, mr_hbm, ms_hbm, mc_hbm, g_ref, raw, ct_ref, xb, qf, means, image, sems):
     fields, nx, ny, modes = x_hbm.shape
 
     def copy(i):
         return pltpu.make_async_copy(x_hbm.at[:, i], xb.at[i], sems.at[i])
 
+    coefficients = [
+        pltpu.make_async_copy(ref, means.at[j], sems.at[nx + j])
+        for j, ref in enumerate((mu_hbm, mv_hbm, mr_hbm, ms_hbm, mc_hbm))
+    ]
+    for one in coefficients:
+        one.start()
     for i in range(nx):
         copy(i).start()
 
     raw[...] = jnp.zeros_like(raw)
-    for j, value in enumerate(
-        (mu[...] * -0.5, mv[...] * -0.5, mr[...] * -0.5, -ms[...], -0.5 / mr[...], mc[...] * -0.5)
-    ):
+    for one in coefficients:
+        one.wait()
+    u, v, rho, shear_u, stiff = (means[j] for j in range(5))
+    for j, value in enumerate((u * -0.5, v * -0.5, rho * -0.5, -shear_u, -0.5 / rho, stiff * -0.5)):
         raw[j * nx : (j + 1) * nx, 0:ny] = value
     ct_ref[...] = raw[...].T
     qf[0] = jnp.zeros(qf.shape[1:], jnp.float32)
@@ -112,20 +121,21 @@
         out_shape=(
             jax.ShapeDtypeStruct((modes, 2 * modes), jnp.float32),
             jax.ShapeDtypeStruct((128, 128), jnp.float32),
+            jax.ShapeDtypeStruct((128, 128), jnp.float32),
         ),
-        in_specs=[pl.BlockSpec(memory_space=pltpu.HBM)] + [pl.BlockSpec(memory_space=pltpu.VMEM)] * 5,
-        out_specs=(pl.BlockSpec(memory_space=pltpu.VMEM),) * 2,
+        in_specs=[pl.BlockSpec(memory_space=pltpu.HBM)] * 6,
+        out_specs=(pl.BlockSpec(memory_space=pltpu.VMEM),) * 3,
         scratch_shapes=[
             pltpu.VMEM((nx, fields, ny, modes), jnp.bfloat16),
             pltpu.VMEM((nx + 2, fields, ny + 2 * pad, modes), jnp.float32),
-            pltpu.VMEM((128, 128), jnp.float32),
+            pltpu.VMEM((5, nx, ny), jnp.float32),
             pltpu.VMEM((fields * ny, 2 * modes), jnp.bfloat16),
-            pltpu.SemaphoreType.DMA((nx,)),
+            pltpu.SemaphoreType.DMA((nx + 5,)),
         ],
         compiler_params=pltpu.CompilerParams(vmem_limit_bytes=20 << 20),
         cost_estimate=pl.CostEstimate(flops=20 * 10**9, transcendentals=0, bytes_accessed=10**7),
         name="interior",
-    )(snapshots, *means)
+    )(*(pltpu.with_memory_space_constraint(a, pltpu.HBM) for a in (snapshots, *means)))
 
 
 def split(value):
@@ -135,16 +145,80 @@
     return high, middle, (rest - middle.astype(jnp.float32)).astype(jnp.bfloat16)
 
 
+def outline_kernel(x_hbm, eig_ref, mv_hbm, mr_hbm, mc_hbm, own_ref, head_y, tail_y, head_x, tail_x, low, high, means, sems):
+    fields, nx, ny, modes = x_hbm.shape
+    copies = [
+        pltpu.make_async_copy(x_hbm.at[:, :, 0:strip], low, sems.at[0]),
+        pltpu.make_async_copy(x_hbm.at[:, :, ny - strip : ny], high, sems.at[1]),
+        pltpu.make_async_copy(x_hbm.at[:, 0], head_x, sems.at[2]),
+        pltpu.make_async_copy(x_hbm.at[:, nx - 1], tail_x, sems.at[3]),
+        pltpu.make_async_copy(mv_hbm, means.at[0], sems.at[4]),
+        pltpu.make_async_copy(mr_hbm, means.at[1], sems.at[5]),
+        pltpu.make_async_copy(mc_hbm, means.at[2], sems.at[6]),
+    ]
+    for copy in copies:
+        copy.start()
+    for t in range(own_ref.shape[0]):
+        own_ref[t] = eig_ref[...]
+    rows = lax.broadcasted_iota(jnp.int32, (nx, nx * strip), 0)
+    cells = lax.broadcasted_iota(jnp.int32, (nx, nx * strip), 1)
+    lanes = lax.broadcasted_iota(jnp.int32, (nx, modes), 1)
+    for at, held, source, edge in ((0, low, head_y, 0), (1, high, tail_y, strip - 1)):
+        chosen = jnp.where(cells == rows * strip + edge, 1.0, 0.0).astype(jnp.bfloat16)
+        copies[at].wait()
+        for f in range(fields):
+            picked = jnp.dot(
+                chosen, held[f].reshape(nx * strip, modes), preferred_element_type=jnp.float32
+            )
+            source[f] = picked.astype(jnp.bfloat16)
+    for copy in copies[4:]:
+        copy.wait()
+    v, rho, stiff = (means[j, :, 0:1] for j in range(3))
+    packed = jnp.zeros((nx, modes), jnp.float32)
+    for j, value in enumerate((v * -0.5, rho * -0.5, -0.5 / rho, stiff * -0.5)):
+        for p, part in enumerate(split(value)):
+            packed = jnp.where(lanes == 3 * j + p, part.astype(jnp.float32), packed)
+    head_y[fields] = packed.astype(jnp.bfloat16)
+    copies[2].wait()
+    copies[3].wait()
+
+
+def outline(snapshots, eig_rows, tiles_n, mean_v, mean_rho, sound):
+    fields, nx, ny, modes = snapshots.shape
+    narrow = jnp.bfloat16
+    in_hbm = [pltpu.with_memory_space_constraint(a, pltpu.HBM) for a in (snapshots, mean_v, mean_rho, sound)]
+    hbm, vmem = pl.BlockSpec(memory_space=pltpu.HBM), pl.BlockSpec(memory_space=pltpu.VMEM)
+    return pl.pallas_call(
+        outline_kernel,
+        out_shape=(
+            jax.ShapeDtypeStruct((tiles_n,) + eig_rows.shape, narrow),
+            jax.ShapeDtypeStruct((fields + 1, nx, modes), narrow),
+            jax.ShapeDtypeStruct((fields, nx, modes), narrow),
+            jax.ShapeDtypeStruct((fields, ny, modes), narrow),
+            jax.ShapeDtypeStruct((fields, ny, modes), narrow),
+        ),
+        in_specs=[hbm, vmem, hbm, hbm, hbm],
+        out_specs=(vmem,) * 5,
+        scratch_shapes=[
+            pltpu.VMEM((fields, nx, strip, modes), narrow),
+            pltpu.VMEM((fields, nx, strip, modes), narrow),
+            pltpu.VMEM((3, nx, ny), jnp.float32),
+            pltpu.SemaphoreType.DMA((7,)),
+        ],
+        compiler_params=pltpu.CompilerParams(vmem_limit_bytes=8 << 20),
+        name="outline",
+    )(in_hbm[0], eig_rows, *in_hbm[1:])
+
+
 def contract(left, right):
     return lax.dot_general(left, right, (((0,), (0,)), ((), ())), preferred_element_type=jnp.float32)
 
 
 def finish_kernel(
-    scale, g_ref, ct_ref, head_x, tail_x, from_west, from_east, tail_y, from_north,
-    mv, mr, mc, vt_ref, out_ref
+    scale, order, g_ref, raw, ct_ref, head_x, tail_x, from_west, from_east, tail_y, from_north, vt_ref, out_ref
 ):
     modes = g_ref.shape[0]
-    ny = head_x.shape[2]
+    ny = head_x.shape[1]
     nx = tail_y.shape[1]
     total = g_ref[:, 0:modes] + g_ref[:, modes : 2 * modes]
 
@@ -167,25 +241,22 @@
         return added
 
     def plane(ref):
-        return lambda f: ref[f, 0].astype(jnp.float32)
+        return lambda f: ref[f].astype(jnp.float32)
 
     def column_x(i):
         return tuple(ct_ref[0:ny, j * nx + i : j * nx + i + 1] for j in (0, 2, 4, 5))
 
-    total += side(lambda f: head_x[f, 0], plane(from_west), column_x(0), 1, 2, -1.0)
-    total += side(lambda f: tail_x[f, 0], plane(from_east), column_x(nx - 1), 1, 2, 1.0)
-
-    own_column = tuple(
-        c for c in (mv[:, ny - 1 : ny] * -0.5, mr[:, ny - 1 : ny] * -0.5, -0.5 / mr[:, ny - 1 : ny], mc[:, ny - 1 : ny] * -0.5)
-    )
+    total += side(lambda f: head_x[f], plane(from_west), column_x(0), 1, 2, -1.0)
+    total += side(lambda f: tail_x[f], plane(from_east), column_x(nx - 1), 1, 2, 1.0)
+
+    own_column = tuple(raw[j * nx : (j + 1) * nx, ny - 1 : ny] for j in (1, 2, 4, 5))
     packed = from_north[5].astype(jnp.float32)
     other_column = tuple(
         packed[:, 3 * j : 3 * j + 1] + packed[:, 3 * j + 1 : 3 * j + 2] + packed[:, 3 * j + 2 : 3 * j + 3]
         for j in range(4)
     )
-    wide = lambda ref: (lambda f: ref[f].astype(jnp.float32))
-    total += side(lambda f: tail_y[f], wide(from_north), own_column, 2, 1, 1.0)
-    total += side(lambda f: from_north[f], wide(tail_y), other_column, 2, 1, -1.0)
+    total += side(lambda f: tail_y[f], plane(from_north), own_column, 2, 1, 1.0)
+    total += side(lambda f: from_north[f], plane(tail_y), other_column, 2, 1, -1.0)
 
     vt = vt_ref[...]
     right = None
@@ -196,15 +267,15 @@
     for part in split(right):
         one = jnp.dot(vt, part, preferred_element_type=jnp.float32)
         both = one if both is None else both + one
-    out_ref[...] = (both * scale).astype(out_ref.dtype)
-
-
-def finish(scale, *operands):
-    import functools
-
+    rows = modes // len(order)
+    for place, tile in enumerate(order):
+        out_ref[place * rows : (place + 1) * rows] = both[tile * rows : (tile + 1) * rows] * scale
+
+
+def finish(scale, order, *operands):
     modes = operands[-1].shape[0]
     return pl.pallas_call(
-        functools.partial(finish_kernel, scale),
+        functools.partial(finish_kernel, scale, order),
         out_shape=jax.ShapeDtypeStruct((modes, modes), jnp.float32),
         in_specs=[pl.BlockSpec(memory_space=pltpu.VMEM)] * len(operands),
         out_specs=pl.BlockSpec(memory_space=pltpu.VMEM),
@@ -213,13 +284,6 @@
     )(*operands)
 
 
-def pieces(value):
-    high = lax.reduce_precision(value, 8, 7)
-    rest = value - high
-    middle = lax.reduce_precision(rest, 8, 7)
-    return [high, middle, rest - middle]
-
-
 def body(snapshots, eig_columns, mean_u, mean_v, mean_rho, mean_shear, sound):
     sections = lax.axis_size("sec")
     tiles_n = lax.axis_size("tile")
@@ -227,27 +291,29 @@
     rows = modes // tiles_n
     scale = float(fields * nx * ny * sections * tiles_n) ** (-0.5)
 
-    first = (mean_v[:, 0], mean_rho[:, 0], sound[:, 0])
-    sent = [first[0] * -0.5, first[1] * -0.5, -0.5 / first[1], first[2] * -0.5]
-    packed = jnp.stack([p for value in sent for p in pieces(value)], axis=-1)
-    packed = jnp.pad(packed, ((0, 0), (0, modes - packed.shape[1])))
-    head_y = jnp.concatenate([snapshots[:, :, 0], packed[None].astype(jnp.bfloat16)])
-    tail_y = snapshots[:, :, ny - 1]
+    own, head_y, tail_y, head_x, tail_x = outline(
+        snapshots, eig_columns.T, tiles_n, mean_v, mean_rho, sound
+    )
+    vt = lax.all_to_all(own, "tile", 0, 0, tiled=True).reshape(modes, modes)
     from_north = lax.ppermute(head_y, "tile", [(i + 1, i) for i in range(tiles_n - 1)])
-    own = jnp.broadcast_to(eig_columns.T[None], (tiles_n, rows, modes))
-    vt = lax.all_to_all(own, "tile", 0, 0, tiled=True).reshape(modes, modes)
-    head_x = snapshots[:, :1]
-    tail_x = snapshots[:, nx - 1 :]
     from_west = lax.ppermute(tail_x, "sec", [(i, i + 1) for i in range(sections - 1)])
     from_east = lax.ppermute(head_x, "sec", [(i + 1, i) for i in range(sections - 1)])
 
-    gram, columns = interior(snapshots, mean_u, mean_v, mean_rho, mean_shear, sound)
+    gram, raw, columns = interior(snapshots, mean_u, mean_v, mean_rho, mean_shear, sound)
+    far = 4
+    near = tiles_n // far
+    plane_groups = [[t for t in range(tiles_n) if t // 2 % far == z] for z in range(far)]
+    line_groups = [[plane_groups[z][r] for z in range(far)] for r in range(near)]
+    order = [t for line in line_groups for t in line]
     local = finish(
-        scale, gram, columns, head_x, tail_x, from_west, from_east, tail_y, from_north,
-        mean_v, mean_rho, sound, vt
-    )
-    shares = lax.all_to_all(local.reshape(tiles_n, rows, modes), "tile", 0, 0, tiled=True)
-    term = shares.sum(0)
+        scale, order, gram, raw, columns, head_x, tail_x, from_west, from_east, tail_y, from_north, vt
+    )
+    shares = lax.all_to_all(
+        local.reshape(near, far * rows, modes), "tile", 0, 0, tiled=True, axis_index_groups=plane_groups
+    ).sum(0)
+    term = lax.all_to_all(
+        shares.reshape(far, rows, modes), "tile", 0, 0, tiled=True, axis_index_groups=line_groups
+    ).sum(0)
     terms = lax.all_to_all(
         jnp.broadcast_to(term[None], (sections, rows, modes)), "sec", 0, 0, tiled=True
     )

time: 107 us -> 95.5 us (0.89)
  the two profiles are of different devices: /device:TPU:1 before, /device:TPU:2 now
where the time goes in v2:
time: 95.5 us; the launch traced here: 95 us
  blocking collectives  32.8 us (34%)
  starting transfers between devices  32.3 us (34%)
  Pallas kernels  17.1 us (18%)
  waiting for transfers between devices  10.7 us (11%)
  local copies, waits for them, and re-layouts  1.33 us (1%)
    all_to_all x1, blocking collectives, body(): lax.all_to_all(shares.reshape(far, rows, modes), 'tile', 0, 0, tiled=True...  20.3 us
    all_to_all x1, blocking collectives, body(): lax.all_to_all(local.reshape(near, far * rows, modes), 'tile', 0, 0, tile...  12.6 us
    pallas_call x1, Pallas kernels, interior(): pl.pallas_call(interior_kernel, out_shape=(jax.ShapeDtypeStruct((modes, 2...  12.2 us
    ppermute x1, starting transfers between devices, body(): lax.ppermute(head_y, 'tile', [(i + 1, i) for i in range(tiles_n - 1)])  11.9 us
    all_to_all x1, waiting for transfers between devices, body(): lax.all_to_all(jnp.broadcast_to(term[None], (sections, rows, modes)), 'se...  8.91 us
    all_to_all x1, starting transfers between devices, body(): vt = lax.all_to_all(own, 'tile', 0, 0, tiled=True).reshape(modes, modes)  8.41 us
    all_to_all x1, starting transfers between devices, body(): lax.all_to_all(jnp.broadcast_to(term[None], (sections, rows, modes)), 'se...  7.19 us
    ppermute x1, starting transfers between devices, body(): lax.ppermute(tail_x, 'sec', [(i, i + 1) for i in range(sections - 1)])  3.5 us
  transfers between devices with their start and end apart: 5, of which 2 were waited for; matrix products, arithmetic and copies ran while one was open for 0% of the time, Pallas kernels for 13%

profile of v2, /device:TPU:2, one launch (start us, length us, event | category | flops | bytes accessed | tf_op | source)
XLA Modules:
  0.0 95.0 jit_solution(3909056973597544737)
XLA Ops:
  0.0 0.0 copy-start
  0.0 0.7 copy-done
  0.7 2.3 %outline.1 = (bf16[32,8,256]{2,1,0:T(8,128)(2,1)}, bf16[6,16,256]{2,1,0:T(8,128)(2,1)S(1)}, bf16[5,16,256]{2,1,0:T(8,128)(2,1)S(1)}, bf16[5,96,256]{2,1,0:T(8,128)(2,1)S(1)}, bf16[5,96,256]{2,1,0:T(8,128)(2,1)S(1)}) custom-call(bf16[5,16,96,256]{3,2,1,0:T(8,128)(2,1)} %x_hbm.3, bf16[8,256]{1,0:T(8,128)(2,1)S(1)} %bitcast.7, f32[16,96]{1,0:T(8,128)} %mv_hbm.3, ...), custom_call_target="tpu_custom_call" | custom-call | tf_op jit(solution)/shard_map/outline/pallas_call | solution.py:191
  3.0 3.5 %collective-permute-start = (bf16[5,96,256]{2,1,0:T(8,128)(2,1)S(1)}, bf16[5,96,256]{2,1,0:T(8,128)(2,1)S(1)}, u32[]{:S(2)}, u32[]{:S(2)}) collective-permute-start(bf16[5,96,256]{2,1,0:T(8,128)(2,1)S(1)} %get-tuple-element.17.tail_x), channel_id=1, source_target_pairs={{0,32},{32,64},{64,96},{96,128},{128,160},{160,192},{192,224},{224... | collective-permute-start | bytes 737288 | tf_op jit(solution)/shard_map/ppermute | solution.py:299
  6.5 1.3 %collective-permute-start.1 = (bf16[5,96,256]{2,1,0:T(8,128)(2,1)S(1)}, bf16[5,96,256]{2,1,0:T(8,128)(2,1)S(1)}, u32[]{:S(2)}, u32[]{:S(2)}) collective-permute-start(bf16[5,96,256]{2,1,0:T(8,128)(2,1)S(1)} %get-tuple-element.16.head_x), channel_id=1, source_target_pairs={{32,0},{64,32},{96,64},{128,96},{160,128},{192,160},{224,192},{256... | collective-permute-start | bytes 737288 | tf_op jit(solution)/shard_map/ppermute | solution.py:300
  7.8 11.9 %collective-permute-start.2 = (bf16[6,16,256]{2,1,0:T(8,128)(2,1)S(1)}, bf16[6,16,256]{2,1,0:T(8,128)(2,1)S(1)}, u32[]{:S(2)}, u32[]{:S(2)}) collective-permute-start(bf16[6,16,256]{2,1,0:T(8,128)(2,1)S(1)} %get-tuple-element.19), channel_id=1, source_target_pairs={{1,0},{2,1},{3,2},{4,3},{5,4},{6,5},{7,6},{8,7},{9,8},{10,9},{11,1... | collective-permute-start | bytes 147464 | tf_op jit(solution)/shard_map/ppermute | solution.py:298
  19.7 8.4 %all-to-all-start = ((bf16[32,8,256]{2,1,0:T(8,128)(2,1)}), bf16[32,8,256]{2,1,0:T(8,128)(2,1)S(1)}, u32[]{:S(2)}, u32[]{:S(2)}) async-start(bf16[32,8,256]{2,1,0:T(8,128)(2,1)} %get-tuple-element.20), calls=%async_computation | async-start | bytes 262144 | tf_op jit(solution)/shard_map/all_to_all | solution.py:297
  28.1 12.2 %interior.1 = (f32[256,512]{1,0:T(8,128)S(1)}, f32[128,128]{1,0:T(8,128)S(1)}, f32[128,128]{1,0:T(8,128)S(1)}) custom-call(bf16[5,16,96,256]{3,2,1,0:T(8,128)(2,1)} %x_hbm.3, f32[16,96]{1,0:T(8,128)} %mu_hbm.1, f32[16,96]{1,0:T(8,128)} %mv_hbm.3, f32[16,96]{1,0:T(8,128)} %mr_hbm.3, f32[16,96]{1,0:T(8,128)} %ms_hbm.1, f32[16,96]{1,0:T(8,128)} %mc_hbm.3), custom_call_target="tpu_custom_call" | custom-call | flops 20000000000 | bytes 10000000 | tf_op jit(solution)/shard_map/interior/pallas_call | solution.py:119
  40.3 0.0 collective-permute-done.2.from_north
  40.3 0.0 collective-permute-done.from_west
  40.3 0.0 collective-permute-done.1.from_east
  40.4 1.8 %all-to-all-done = bf16[32,8,256]{2,1,0:T(8,128)(2,1)S(1)} async-done(((bf16[32,8,256]{2,1,0:T(8,128)(2,1)}), bf16[32,8,256]{2,1,0:T(8,128)(2,1)S(1)}, u32[]{:S(2)}, u32[]{:S(2)}) %all-to-all-start) | async-done | bytes 131104 | tf_op jit(solution)/shard_map/all_to_all | solution.py:297
  42.1 2.6 %finish.1 = f32[256,256]{1,0:T(8,128)S(1)} custom-call(f32[256,512]{1,0:T(8,128)S(1)} %get-tuple-element.13.g_ref, f32[128,128]{1,0:T(8,128)S(1)} %get-tuple-element.14.raw, f32[128,128]{1,0:T(8,128)S(1)} %get-tuple-element.15.ct_ref, bf16[5,96,256]{2,1,0:T(8,128)(2,1)S(1)} %get-tuple-element.16.head_x, bf16[5,96,256]{2,1,0:T(8,128)(2,1)S(1)} %get-tuple-element.17.tail_x, ...), custom_call_target="tpu_custom_call" | custom-call | tf_op jit(solution)/shard_map/finish/pallas_call | solution.py:277
  44.7 12.6 %all_to_all.20 = f32[8,32,256]{2,1,0:T(8,128)S(1)} all-to-all(f32[8,32,256]{2,1,0:T(8,128)S(1)} %bitcast.5), channel_id=1, replica_groups={{0,1,8,9,16,17,24,25},{2,3,10,11,18,19,26,27},{4,5,12,13,20,21,28,29},{..., dimensions={0} | all-to-all | bytes 524288 | tf_op jit(solution)/shard_map/all_to_all | solution.py:311
  57.3 20.3 %all_to_all.21 = f32[4,8,256]{2,1,0:T(8,128)S(1)} all-to-all(f32[4,8,256]{2,1,0:T(8,128)S(1)} %bitcast.8), channel_id=1, replica_groups={{0,2,4,6},{1,3,5,7},{8,10,12,14},{9,11,13,15},{16,18,20,22},{17,19,21,2..., dimensions={0} | all-to-all | bytes 65536 | tf_op jit(solution)/shard_map/all_to_all | solution.py:314
  77.6 0.6 broadcast_in_dim.23
  78.2 7.2 %all-to-all-start.3 = ((f32[16,8,256]{2,1,0:T(8,128)}), f32[16,8,256]{2,1,0:T(8,128)S(1)}, u32[]{:S(2)}, u32[]{:S(2)}) async-start(f32[16,8,256]{2,1,0:T(8,128)} %broadcast_in_dim.23), calls=%async_computation.3 | async-start | bytes 262144 | tf_op jit(solution)/shard_map/all_to_all | solution.py:317
  85.4 8.9 %all-to-all-done.3 = f32[16,8,256]{2,1,0:T(8,128)S(1)} async-done(((f32[16,8,256]{2,1,0:T(8,128)}), f32[16,8,256]{2,1,0:T(8,128)S(1)}, u32[]{:S(2)}, u32[]{:S(2)}) %all-to-all-start.3) | async-done | bytes 131104 | tf_op jit(solution)/shard_map/all_to_all | solution.py:317
  94.4 0.7 select_reduce_fusion
  (3 shorter events, 0.0 us)
Async XLA Ops:
  0.0 0.7 copy-start
  3.0 37.3 %collective-permute-start = (bf16[5,96,256]{2,1,0:T(8,128)(2,1)S(1)}, bf16[5,96,256]{2,1,0:T(8,128)(2,1)S(1)}, u32[]{:S(2)}, u32[]{:S(2)}) collective-permute-start(bf16[5,96,256]{2,1,0:T(8,128)(2,1)S(1)} %get-tuple-element.17.tail_x), channel_id=1, source_target_pairs={{0,32},{32,64},{64,96},{96,128},{128,160},{160,192},{192,224},{224... | collective-permute-start | bytes 737288 | tf_op jit(solution)/shard_map/ppermute | solution.py:299
  6.5 33.8 %collective-permute-start.1 = (bf16[5,96,256]{2,1,0:T(8,128)(2,1)S(1)}, bf16[5,96,256]{2,1,0:T(8,128)(2,1)S(1)}, u32[]{:S(2)}, u32[]{:S(2)}) collective-permute-start(bf16[5,96,256]{2,1,0:T(8,128)(2,1)S(1)} %get-tuple-element.16.head_x), channel_id=1, source_target_pairs={{32,0},{64,32},{96,64},{128,96},{160,128},{192,160},{224,192},{256... | collective-permute-start | bytes 737288 | tf_op jit(solution)/shard_map/ppermute | solution.py:300
  7.8 32.5 %collective-permute-start.2 = (bf16[6,16,256]{2,1,0:T(8,128)(2,1)S(1)}, bf16[6,16,256]{2,1,0:T(8,128)(2,1)S(1)}, u32[]{:S(2)}, u32[]{:S(2)}) collective-permute-start(bf16[6,16,256]{2,1,0:T(8,128)(2,1)S(1)} %get-tuple-element.19), channel_id=1, source_target_pairs={{1,0},{2,1},{3,2},{4,3},{5,4},{6,5},{7,6},{8,7},{9,8},{10,9},{11,1... | collective-permute-start | bytes 147464 | tf_op jit(solution)/shard_map/ppermute | solution.py:298
  19.7 22.5 %all-to-all-start = ((bf16[32,8,256]{2,1,0:T(8,128)(2,1)}), bf16[32,8,256]{2,1,0:T(8,128)(2,1)S(1)}, u32[]{:S(2)}, u32[]{:S(2)}) async-start(bf16[32,8,256]{2,1,0:T(8,128)(2,1)} %get-tuple-element.20), calls=%async_computation | async-start | bytes 262144 | tf_op jit(solution)/shard_map/all_to_all | solution.py:297
  78.2 16.1 %all-to-all-start.3 = ((f32[16,8,256]{2,1,0:T(8,128)}), f32[16,8,256]{2,1,0:T(8,128)S(1)}, u32[]{:S(2)}, u32[]{:S(2)}) async-start(f32[16,8,256]{2,1,0:T(8,128)} %broadcast_in_dim.23), calls=%async_computation.3 | async-start | bytes 262144 | tf_op jit(solution)/shard_map/all_to_all | solution.py:317

commit v3 on v2

--- a/solution.py
+++ b/solution.py
@@ -6,6 +6,7 @@
 from jax.experimental import pallas as pl
 from jax.experimental.pallas import tpu as pltpu
 from jax.sharding import PartitionSpec as P
+
 
 viscosity = 0.002
 pad = 8
@@ -145,7 +146,27 @@
     return high, middle, (rest - middle.astype(jnp.float32)).astype(jnp.bfloat16)
 
 
-def outline_kernel(x_hbm, eig_ref, mv_hbm, mr_hbm, mc_hbm, own_ref, head_y, tail_y, head_x, tail_x, low, high, means, sems):
+def repeat_kernel(eig_hbm, own_ref, held, sem):
+    copy = pltpu.make_async_copy(eig_hbm, held, sem)
+    copy.start()
+    copy.wait()
+    for t in range(own_ref.shape[0]):
+        own_ref[t] = held[...]
+
+
+def repeat(eig_rows, times):
+    return pl.pallas_call(
+        repeat_kernel,
+        out_shape=jax.ShapeDtypeStruct((times,) + eig_rows.shape, eig_rows.dtype),
+        in_specs=[pl.BlockSpec(memory_space=pltpu.HBM)],
+        out_specs=pl.BlockSpec(memory_space=pltpu.VMEM),
+        scratch_shapes=[pltpu.VMEM(eig_rows.shape, eig_rows.dtype), pltpu.SemaphoreType.DMA],
+        compiler_params=pltpu.CompilerParams(vmem_limit_bytes=2 << 20),
+        name="repeat",
+    )(pltpu.with_memory_space_constraint(eig_rows, pltpu.HBM))
+
+
+def outline_kernel(x_hbm, mv_hbm, mr_hbm, mc_hbm, head_y, tail_y, head_x, tail_x, low, high, means, sems):
     fields, nx, ny, modes = x_hbm.shape
     copies = [
         pltpu.make_async_copy(x_hbm.at[:, :, 0:strip], low, sems.at[0]),
@@ -158,8 +179,6 @@
     ]
     for copy in copies:
         copy.start()
-    for t in range(own_ref.shape[0]):
-        own_ref[t] = eig_ref[...]
     rows = lax.broadcasted_iota(jnp.int32, (nx, nx * strip), 0)
     cells = lax.broadcasted_iota(jnp.int32, (nx, nx * strip), 1)
     lanes = lax.broadcasted_iota(jnp.int32, (nx, modes), 1)
@@ -183,7 +202,7 @@
     copies[3].wait()
 
 
-def outline(snapshots, eig_rows, tiles_n, mean_v, mean_rho, sound):
+def outline(snapshots, mean_v, mean_rho, sound):
     fields, nx, ny, modes = snapshots.shape
     narrow = jnp.bfloat16
     in_hbm = [pltpu.with_memory_space_constraint(a, pltpu.HBM) for a in (snapshots, mean_v, mean_rho, sound)]
@@ -191,14 +210,13 @@
     return pl.pallas_call(
         outline_kernel,
         out_shape=(
-            jax.ShapeDtypeStruct((tiles_n,) + eig_rows.shape, narrow),
             jax.ShapeDtypeStruct((fields + 1, nx, modes), narrow),
             jax.ShapeDtypeStruct((fields, nx, modes), narrow),
             jax.ShapeDtypeStruct((fields, ny, modes), narrow),
             jax.ShapeDtypeStruct((fields, ny, modes), narrow),
         ),
-        in_specs=[hbm, vmem, hbm, hbm, hbm],
-        out_specs=(vmem,) * 5,
+        in_specs=[hbm] * 4,
+        out_specs=(vmem,) * 4,
         scratch_shapes=[
             pltpu.VMEM((fields, nx, strip, modes), narrow),
             pltpu.VMEM((fields, nx, strip, modes), narrow),
@@ -207,7 +225,7 @@
         ],
         compiler_params=pltpu.CompilerParams(vmem_limit_bytes=8 << 20),
         name="outline",
-    )(in_hbm[0], eig_rows, *in_hbm[1:])
+    )(*in_hbm)
 
 
 def contract(left, right):
@@ -215,14 +233,14 @@
 
 
 def finish_kernel(
-    scale, order, g_ref, raw, ct_ref, head_x, tail_x, from_west, from_east, tail_y, from_north, vt_ref, out_ref
+    scale, gathered, order, g_ref, raw, ct_ref, head_x, tail_x, from_west, from_east, tail_y, from_north, vt_ref, out_ref, placed
 ):
     modes = g_ref.shape[0]
     ny = head_x.shape[1]
     nx = tail_y.shape[1]
     total = g_ref[:, 0:modes] + g_ref[:, modes : 2 * modes]
 
-    def side(own, other, column, along, cross, sign):
+    def side(own, other, column, along, sign):
         half_c, half_rho, half_inverse, half_sound = (sign * c for c in column)
         spread_c = viscosity + half_c
         images = [
@@ -246,8 +264,8 @@
     def column_x(i):
         return tuple(ct_ref[0:ny, j * nx + i : j * nx + i + 1] for j in (0, 2, 4, 5))
 
-    total += side(lambda f: head_x[f], plane(from_west), column_x(0), 1, 2, -1.0)
-    total += side(lambda f: tail_x[f], plane(from_east), column_x(nx - 1), 1, 2, 1.0)
+    total += side(lambda f: head_x[f], plane(from_west), column_x(0), 1, -1.0)
+    total += side(lambda f: tail_x[f], plane(from_east), column_x(nx - 1), 1, 1.0)
 
     own_column = tuple(raw[j * nx : (j + 1) * nx, ny - 1 : ny] for j in (1, 2, 4, 5))
     packed = from_north[5].astype(jnp.float32)
@@ -255,10 +273,13 @@
         packed[:, 3 * j : 3 * j + 1] + packed[:, 3 * j + 1 : 3 * j + 2] + packed[:, 3 * j + 2 : 3 * j + 3]
         for j in range(4)
     )
-    total += side(lambda f: tail_y[f], plane(from_north), own_column, 2, 1, 1.0)
-    total += side(lambda f: from_north[f], plane(tail_y), other_column, 2, 1, -1.0)
-
-    vt = vt_ref[...]
+    total += side(lambda f: tail_y[f], plane(from_north), own_column, 2, 1.0)
+    total += side(lambda f: from_north[f], plane(tail_y), other_column, 2, -1.0)
+
+    rows = modes // len(order)
+    for place, tile in enumerate(gathered):
+        placed[tile * rows : (tile + 1) * rows] = vt_ref[place].astype(jnp.float32)
+    vt = placed[...].astype(jnp.bfloat16)
     right = None
     for part in split(total):
         one = lax.dot_general(part, vt, (((1,), (1,)), ((), ())), preferred_element_type=jnp.float32)
@@ -267,18 +288,18 @@
     for part in split(right):
         one = jnp.dot(vt, part, preferred_element_type=jnp.float32)
         both = one if both is None else both + one
-    rows = modes // len(order)
     for place, tile in enumerate(order):
         out_ref[place * rows : (place + 1) * rows] = both[tile * rows : (tile + 1) * rows] * scale
 
 
-def finish(scale, order, *operands):
-    modes = operands[-1].shape[0]
+def finish(scale, gathered, order, *operands):
+    modes = operands[-1].shape[-1]
     return pl.pallas_call(
-        functools.partial(finish_kernel, scale, order),
+        functools.partial(finish_kernel, scale, gathered, order),
         out_shape=jax.ShapeDtypeStruct((modes, modes), jnp.float32),
         in_specs=[pl.BlockSpec(memory_space=pltpu.VMEM)] * len(operands),
         out_specs=pl.BlockSpec(memory_space=pltpu.VMEM),
+        scratch_shapes=[pltpu.VMEM((modes, modes), jnp.float32)],
         compiler_params=pltpu.CompilerParams(vmem_limit_bytes=12 << 20),
         name="finish",
     )(*operands)
@@ -291,22 +312,29 @@
     rows = modes // tiles_n
     scale = float(fields * nx * ny * sections * tiles_n) ** (-0.5)
 
-    own, head_y, tail_y, head_x, tail_x = outline(
-        snapshots, eig_columns.T, tiles_n, mean_v, mean_rho, sound
-    )
-    vt = lax.all_to_all(own, "tile", 0, 0, tiled=True).reshape(modes, modes)
+    far = 4
+    near = tiles_n // far
+    wide = near // 2
+    gathered = [
+        ((x + wide // 2) % wide * far + (z + far // 2) % far) * 2 + core
+        for x in range(wide)
+        for z in range(far)
+        for core in range(2)
+    ]
+    arrived = [(s + sections - 2) % sections for s in range(sections)]
+    own = repeat(eig_columns.T, tiles_n)
+    vt = lax.all_to_all(own, "tile", 0, 0, tiled=True, axis_index_groups=[gathered])
+    head_y, tail_y, head_x, tail_x = outline(snapshots, mean_v, mean_rho, sound)
     from_north = lax.ppermute(head_y, "tile", [(i + 1, i) for i in range(tiles_n - 1)])
     from_west = lax.ppermute(tail_x, "sec", [(i, i + 1) for i in range(sections - 1)])
     from_east = lax.ppermute(head_x, "sec", [(i + 1, i) for i in range(sections - 1)])
 
     gram, raw, columns = interior(snapshots, mean_u, mean_v, mean_rho, mean_shear, sound)
-    far = 4
-    near = tiles_n // far
-    plane_groups = [[t for t in range(tiles_n) if t // 2 % far == z] for z in range(far)]
+    plane_groups = [[t for t in range(tiles_n) if t // 2 % far == (z + far // 2) % far] for z in range(far)]
     line_groups = [[plane_groups[z][r] for z in range(far)] for r in range(near)]
     order = [t for line in line_groups for t in line]
     local = finish(
-        scale, order, gram, raw, columns, head_x, tail_x, from_west, from_east, tail_y, from_north, vt
+        scale, gathered, order, gram, raw, columns, head_x, tail_x, from_west, from_east, tail_y, from_north, vt
     )
     shares = lax.all_to_all(
         local.reshape(near, far * rows, modes), "tile", 0, 0, tiled=True, axis_index_groups=plane_groups
@@ -315,9 +343,9 @@
         shares.reshape(far, rows, modes), "tile", 0, 0, tiled=True, axis_index_groups=line_groups
     ).sum(0)
     terms = lax.all_to_all(
-        jnp.broadcast_to(term[None], (sections, rows, modes)), "sec", 0, 0, tiled=True
+        jnp.broadcast_to(term[None], (sections, rows, modes)), "sec", 0, 0, tiled=True, axis_index_groups=[arrived]
     )
-    upstream = jnp.arange(sections) <= lax.axis_index("sec")
+    upstream = jnp.array(arrived) <= lax.axis_index("sec")
     return jnp.where(upstream[:, None, None], terms, 0.0).sum(0)[None]
 
 

time: 95.5 us -> 89.4 us (0.936)
  the two profiles are of different devices: /device:TPU:2 before, /device:TPU:8 now
where the time goes in v3:
time: 89.4 us; the launch traced here: 89 us
  starting transfers between devices  40.5 us (45%)
  blocking collectives  24.2 us (27%)
  Pallas kernels  17.8 us (20%)
  waiting for transfers between devices  4.95 us (6%)
    all_to_all x1, starting transfers between devices, body(): lax.all_to_all(own, 'tile', 0, 0, tiled=True, axis_index_groups=[gathered])  22.7 us
    all_to_all x1, blocking collectives, body(): lax.all_to_all(shares.reshape(far, rows, modes), 'tile', 0, 0, tiled=True...  14.3 us
    pallas_call x1, Pallas kernels, interior(): pl.pallas_call(interior_kernel, out_shape=(jax.ShapeDtypeStruct((modes, 2...  12.2 us
    all_to_all x1, blocking collectives, body(): lax.all_to_all(local.reshape(near, far * rows, modes), 'tile', 0, 0, tile...  9.91 us
    all_to_all x1, starting transfers between devices, body(): lax.all_to_all(jnp.broadcast_to(term[None], (sections, rows, modes)), 'se...  7.49 us
    ppermute x1, starting transfers between devices, body(): lax.ppermute(head_x, 'sec', [(i + 1, i) for i in range(sections - 1)])  5.52 us
    all_to_all x1, waiting for transfers between devices, body(): lax.all_to_all(jnp.broadcast_to(term[None], (sections, rows, modes)), 'se...  4.94 us
    ppermute x1, starting transfers between devices, body(): lax.ppermute(tail_x, 'sec', [(i, i + 1) for i in range(sections - 1)])  3.48 us
  transfers between devices with their start and end apart: 5, of which 1 were waited for; matrix products, arithmetic and copies ran while one was open for 0% of the time, Pallas kernels for 15%

profile of v3, /device:TPU:8, one launch (start us, length us, event | category | flops | bytes accessed | tf_op | source)
XLA Modules:
  0.0 89.0 jit_solution(7118051488709476583)
XLA Ops:
  0.0 1.7 %outline.1 = (bf16[6,16,256]{2,1,0:T(8,128)(2,1)S(1)}, bf16[5,16,256]{2,1,0:T(8,128)(2,1)S(1)}, bf16[5,96,256]{2,1,0:T(8,128)(2,1)S(1)}, bf16[5,96,256]{2,1,0:T(8,128)(2,1)S(1)}) custom-call(bf16[5,16,96,256]{3,2,1,0:T(8,128)(2,1)} %x_hbm.3, f32[16,96]{1,0:T(8,128)} %mv_hbm.3, f32[16,96]{1,0:T(8,128)} %mr_hbm.3, f32[16,96]{1,0:T(8,128)} %mc_hbm.3), custom_call_target="tpu_custom_call" | custom-call | tf_op jit(solution)/shard_map/outline/pallas_call | solution.py:210
  1.7 3.5 %collective-permute-start = (bf16[5,96,256]{2,1,0:T(8,128)(2,1)S(1)}, bf16[5,96,256]{2,1,0:T(8,128)(2,1)S(1)}, u32[]{:S(2)}, u32[]{:S(2)}) collective-permute-start(bf16[5,96,256]{2,1,0:T(8,128)(2,1)S(1)} %get-tuple-element.16.tail_x), channel_id=1, source_target_pairs={{0,32},{32,64},{64,96},{96,128},{128,160},{160,192},{192,224},{224... | collective-permute-start | bytes 737288 | tf_op jit(solution)/shard_map/ppermute | solution.py:329
  5.2 5.5 %collective-permute-start.1 = (bf16[5,96,256]{2,1,0:T(8,128)(2,1)S(1)}, bf16[5,96,256]{2,1,0:T(8,128)(2,1)S(1)}, u32[]{:S(2)}, u32[]{:S(2)}) collective-permute-start(bf16[5,96,256]{2,1,0:T(8,128)(2,1)S(1)} %get-tuple-element.15.head_x), channel_id=1, source_target_pairs={{32,0},{64,32},{96,64},{128,96},{160,128},{192,160},{224,192},{256... | collective-permute-start | bytes 737288 | tf_op jit(solution)/shard_map/ppermute | solution.py:330
  10.7 1.3 %collective-permute-start.2 = (bf16[6,16,256]{2,1,0:T(8,128)(2,1)S(1)}, bf16[6,16,256]{2,1,0:T(8,128)(2,1)S(1)}, u32[]{:S(2)}, u32[]{:S(2)}) collective-permute-start(bf16[6,16,256]{2,1,0:T(8,128)(2,1)S(1)} %get-tuple-element.18), channel_id=1, source_target_pairs={{1,0},{2,1},{3,2},{4,3},{5,4},{6,5},{7,6},{8,7},{9,8},{10,9},{11,1... | collective-permute-start | bytes 147464 | tf_op jit(solution)/shard_map/ppermute | solution.py:328
  12.0 1.3 %repeat.1 = bf16[32,8,256]{2,1,0:T(8,128)(2,1)} custom-call(bf16[8,256]{1,0:T(8,128)(2,1)} %bitcast.6), custom_call_target="tpu_custom_call" | custom-call | tf_op jit(solution)/shard_map/repeat/pallas_call | solution.py:158
  13.4 22.7 %all-to-all-start = ((bf16[32,8,256]{2,1,0:T(8,128)(2,1)}), bf16[32,8,256]{2,1,0:T(8,128)(2,1)S(1)}, u32[]{:S(2)}, u32[]{:S(2)}) async-start(bf16[32,8,256]{2,1,0:T(8,128)(2,1)} %repeat.1), calls=%async_computation | async-start | bytes 262144 | tf_op jit(solution)/shard_map/all_to_all | solution.py:326
  36.1 0.0 copy-start
  36.1 12.2 %interior.1 = (f32[256,512]{1,0:T(8,128)S(1)}, f32[128,128]{1,0:T(8,128)S(1)}, f32[128,128]{1,0:T(8,128)S(1)}) custom-call(bf16[5,16,96,256]{3,2,1,0:T(8,128)(2,1)} %x_hbm.3, f32[16,96]{1,0:T(8,128)} %mu_hbm.1, f32[16,96]{1,0:T(8,128)} %mv_hbm.3, f32[16,96]{1,0:T(8,128)} %mr_hbm.3, f32[16,96]{1,0:T(8,128)} %ms_hbm.1, f32[16,96]{1,0:T(8,128)} %mc_hbm.3), custom_call_target="tpu_custom_call" | custom-call | flops 20000000000 | bytes 10000000 | tf_op jit(solution)/shard_map/interior/pallas_call | solution.py:120
  48.3 0.0 collective-permute-done.2.from_north
  48.3 0.0 collective-permute-done.from_west
  48.3 0.0 collective-permute-done.1.from_east
  48.4 0.0 all-to-all-done.vt_ref
  48.4 2.6 %finish.1 = f32[256,256]{1,0:T(8,128)S(1)} custom-call(f32[256,512]{1,0:T(8,128)S(1)} %get-tuple-element.12.g_ref, f32[128,128]{1,0:T(8,128)S(1)} %get-tuple-element.13.raw, f32[128,128]{1,0:T(8,128)S(1)} %get-tuple-element.14.ct_ref, bf16[5,96,256]{2,1,0:T(8,128)(2,1)S(1)} %get-tuple-element.15.head_x, bf16[5,96,256]{2,1,0:T(8,128)(2,1)S(1)} %get-tuple-element.16.tail_x, ...), custom_call_target="tpu_custom_call" | custom-call | tf_op jit(solution)/shard_map/finish/pallas_call | solution.py:297
  51.0 9.9 %all_to_all.20 = f32[8,32,256]{2,1,0:T(8,128)S(1)} all-to-all(f32[8,32,256]{2,1,0:T(8,128)S(1)} %bitcast.4), channel_id=1, replica_groups={{4,5,12,13,20,21,28,29},{6,7,14,15,22,23,30,31},{0,1,8,9,16,17,24,25},{..., dimensions={0} | all-to-all | bytes 524288 | tf_op jit(solution)/shard_map/all_to_all | solution.py:339
  60.9 14.3 %all_to_all.21 = f32[4,8,256]{2,1,0:T(8,128)S(1)} all-to-all(f32[4,8,256]{2,1,0:T(8,128)S(1)} %bitcast.5), channel_id=1, replica_groups={{4,6,0,2},{5,7,1,3},{12,14,8,10},{13,15,9,11},{20,22,16,18},{21,23,17,1..., dimensions={0} | all-to-all | bytes 65536 | tf_op jit(solution)/shard_map/all_to_all | solution.py:342
  75.2 0.6 broadcast_in_dim.23
  75.8 7.5 %all-to-all-start.3 = ((f32[16,8,256]{2,1,0:T(8,128)}), f32[16,8,256]{2,1,0:T(8,128)S(1)}, u32[]{:S(2)}, u32[]{:S(2)}) async-start(f32[16,8,256]{2,1,0:T(8,128)} %broadcast_in_dim.23), calls=%async_computation.3 | async-start | bytes 262144 | tf_op jit(solution)/shard_map/all_to_all | solution.py:345
  83.3 0.0 copy-done
  83.3 4.9 %all-to-all-done.3 = f32[16,8,256]{2,1,0:T(8,128)S(1)} async-done(((f32[16,8,256]{2,1,0:T(8,128)}), f32[16,8,256]{2,1,0:T(8,128)S(1)}, u32[]{:S(2)}, u32[]{:S(2)}) %all-to-all-start.3) | async-done | bytes 131104 | tf_op jit(solution)/shard_map/all_to_all | solution.py:345
  88.3 0.7 select_reduce_fusion
  (3 shorter events, 0.0 us)
Async XLA Ops:
  1.7 46.6 %collective-permute-start = (bf16[5,96,256]{2,1,0:T(8,128)(2,1)S(1)}, bf16[5,96,256]{2,1,0:T(8,128)(2,1)S(1)}, u32[]{:S(2)}, u32[]{:S(2)}) collective-permute-start(bf16[5,96,256]{2,1,0:T(8,128)(2,1)S(1)} %get-tuple-element.16.tail_x), channel_id=1, source_target_pairs={{0,32},{32,64},{64,96},{96,128},{128,160},{160,192},{192,224},{224... | collective-permute-start | bytes 737288 | tf_op jit(solution)/shard_map/ppermute | solution.py:329
  5.2 43.2 %collective-permute-start.1 = (bf16[5,96,256]{2,1,0:T(8,128)(2,1)S(1)}, bf16[5,96,256]{2,1,0:T(8,128)(2,1)S(1)}, u32[]{:S(2)}, u32[]{:S(2)}) collective-permute-start(bf16[5,96,256]{2,1,0:T(8,128)(2,1)S(1)} %get-tuple-element.15.head_x), channel_id=1, source_target_pairs={{32,0},{64,32},{96,64},{128,96},{160,128},{192,160},{224,192},{256... | collective-permute-start | bytes 737288 | tf_op jit(solution)/shard_map/ppermute | solution.py:330
  10.7 37.6 %collective-permute-start.2 = (bf16[6,16,256]{2,1,0:T(8,128)(2,1)S(1)}, bf16[6,16,256]{2,1,0:T(8,128)(2,1)S(1)}, u32[]{:S(2)}, u32[]{:S(2)}) collective-permute-start(bf16[6,16,256]{2,1,0:T(8,128)(2,1)S(1)} %get-tuple-element.18), channel_id=1, source_target_pairs={{1,0},{2,1},{3,2},{4,3},{5,4},{6,5},{7,6},{8,7},{9,8},{10,9},{11,1... | collective-permute-start | bytes 147464 | tf_op jit(solution)/shard_map/ppermute | solution.py:328
  13.4 35.0 %all-to-all-start = ((bf16[32,8,256]{2,1,0:T(8,128)(2,1)}), bf16[32,8,256]{2,1,0:T(8,128)(2,1)S(1)}, u32[]{:S(2)}, u32[]{:S(2)}) async-start(bf16[32,8,256]{2,1,0:T(8,128)(2,1)} %repeat.1), calls=%async_computation | async-start | bytes 262144 | tf_op jit(solution)/shard_map/all_to_all | solution.py:326
  36.1 47.2 %copy-start = (s32[16]{0:T(128)S(1)}, s32[16]{0:T(128)}, u32[]{:S(2)}) copy-start(s32[16]{0:T(128)} %constant.10.clone) | copy-start | bytes 196
  75.8 12.4 %all-to-all-start.3 = ((f32[16,8,256]{2,1,0:T(8,128)}), f32[16,8,256]{2,1,0:T(8,128)S(1)}, u32[]{:S(2)}, u32[]{:S(2)}) async-start(f32[16,8,256]{2,1,0:T(8,128)} %broadcast_in_dim.23), calls=%async_computation.3 | async-start | bytes 262144 | tf_op jit(solution)/shard_map/all_to_all | solution.py:345

commit v4 on v3

v4 whole, which is shorter than its diff:
```python
import functools

import jax
import jax.numpy as jnp
from jax import lax
from jax.experimental import pallas as pl
from jax.experimental.pallas import tpu as pltpu
from jax.sharding import PartitionSpec as P


viscosity = 0.002
pad = 8
strip = 16
lanes = 128


def interior_kernel(
    x_hbm, mu_hbm, mv_hbm, mr_hbm, ms_hbm, mc_hbm, g_ref, raw, ct_ref, xb, qf, means, even, odd, sems
):
    fields, nx, ny, modes = x_hbm.shape
    halves = modes // lanes

    def copy(i):
        return pltpu.make_async_copy(x_hbm.at[:, i], xb.at[i], sems.at[i])

    coefficients = [
        pltpu.make_async_copy(ref, means.at[j], sems.at[nx + j])
        for j, ref in enumerate((mu_hbm, mv_hbm, mr_hbm, ms_hbm, mc_hbm))
    ]
    for one in coefficients:
        one.start()
    for i in range(nx):
        copy(i).start()

    raw[...] = jnp.zeros_like(raw)
    qf[0] = jnp.zeros(qf.shape[1:], jnp.float32)
    odd[...] = jnp.zeros_like(odd)
    g_ref[...] = jnp.zeros_like(g_ref)
    for one in coefficients:
        one.wait()
    u, v, rho, shear_u, stiff = (means[j] for j in range(5))
    for j, value in enumerate((u * -0.5, v * -0.5, rho * -0.5, -shear_u, -0.5 / rho, stiff * -0.5)):
        raw[j * nx : (j + 1) * nx, 0:ny] = value
    ct_ref[...] = raw[...].T

    def widen(i):
        edge = jnp.zeros((pad, lanes), jnp.float32)
        for f in range(fields):
            for h in range(halves):
                part = slice(h * lanes, (h + 1) * lanes)
                qf[i + 1, f, h, 0:pad] = edge
                qf[i + 1, f, h, pad + ny : 2 * pad + ny] = edge
                for y in range(0, ny, strip):
                    qf[i + 1, f, h, pad + y : pad + y + strip] = xb[i, f, y : y + strip, part].astype(
                        jnp.float32
                    )

    def apply(i, image):
        zero = jnp.minimum(i, 0)
        turned = pltpu.roll(ct_ref[...], 128 - i, 1)
        for y in range(0, ny, strip):
            column = turned[y : y + strip]
            half_u, half_v, half_rho, shear, half_inverse, half_sound = (
                jnp.broadcast_to(column[:, j * nx : j * nx + 1], (strip, lanes)) for j in range(6)
            )
            east_c, west_c = viscosity + half_u, viscosity - half_u
            north_c, south_c = viscosity + half_v, viscosity - half_v
            top = pad + y
            for h in range(halves):

                def east(f):
                    return qf[i + 2, f, h, top : top + strip]

                def west(f):
                    return qf[i, f, h, top : top + strip]

                def north(f):
                    return qf[i + 1, f, h, pl.ds(zero + top + 1, strip)]

                def south(f):
                    return qf[i + 1, f, h, pl.ds(zero + top - 1, strip)]

                def here(f):
                    return qf[i + 1, f, h, top : top + strip]

                def flow(f):
                    return half_u * (east(f) - west(f)) + half_v * (north(f) - south(f))

                def spread(f):
                    return (
                        east_c * east(f) + west_c * west(f) + north_c * north(f) + south_c * south(f)
                    ) - (4.0 * viscosity) * here(f)

                diverge = (east(1) - west(1)) + (north(2) - south(2))
                images = (
                    flow(0) + half_rho * diverge,
                    spread(1) + shear * here(2) + half_inverse * (east(4) - west(4)),
                    spread(2) + half_inverse * (north(4) - south(4)),
                    spread(3),
                    flow(4) + half_sound * diverge,
                )
                for f in range(fields):
                    high = images[f].astype(jnp.bfloat16)
                    row = f * ny + y
                    image[row : row + strip, h * lanes : (h + 1) * lanes] = high

    def gather(i, image):
        g_ref[...] += lax.dot_general(
            xb[i].reshape(fields * ny, modes),
            image[...],
            (((0,), (0,)), ((), ())),
            preferred_element_type=jnp.float32,
        )

    copy(0).wait()
    widen(0)

    def step(p, carry):
        i = 2 * p
        copy(i + 1).wait()
        widen(i + 1)
        apply(i, even)
        gather(jnp.maximum(i - 1, 0), odd)

        @pl.when(i + 2 < nx)
        def _():
            copy(i + 2).wait()
            widen(i + 2)

        @pl.when(i + 2 == nx)
        def _():
            qf[nx + 1] = jnp.zeros(qf.shape[1:], jnp.float32)

        apply(i + 1, odd)
        gather(i, even)
        return carry

    lax.fori_loop(0, nx // 2, step, 0)
    gather(nx - 1, odd)


def interior(snapshots, *means):
    fields, nx, ny, modes = snapshots.shape
    return pl.pallas_call(
        interior_kernel,
        out_shape=(
            jax.ShapeDtypeStruct((modes, modes), jnp.float32),
            jax.ShapeDtypeStruct((128, 128), jnp.float32),
            jax.ShapeDtypeStruct((128, 128), jnp.float32),
        ),
        in_specs=[pl.BlockSpec(memory_space=pltpu.HBM)] * 6,
        out_specs=(pl.BlockSpec(memory_space=pltpu.VMEM),) * 3,
        scratch_shapes=[
            pltpu.VMEM((nx, fields, ny, modes), jnp.bfloat16),
            pltpu.VMEM((nx + 2, fields, modes // lanes, ny + 2 * pad, lanes), jnp.float32),
            pltpu.VMEM((5, nx, ny), jnp.float32),
            pltpu.VMEM((fields * ny, modes), jnp.bfloat16),
            pltpu.VMEM((fields * ny, modes), jnp.bfloat16),
            pltpu.SemaphoreType.DMA((nx + 5,)),
        ],
        compiler_params=pltpu.CompilerParams(vmem_limit_bytes=20 << 20),
        cost_estimate=pl.CostEstimate(flops=20 * 10**9, transcendentals=0, bytes_accessed=10**7),
        name="interior",
    )(*(pltpu.with_memory_space_constraint(a, pltpu.HBM) for a in (snapshots, *means)))


def split(value):
    high = value.astype(jnp.bfloat16)
    rest = value - high.astype(jnp.float32)
    middle = rest.astype(jnp.bfloat16)
    return high, middle, (rest - middle.astype(jnp.float32)).astype(jnp.bfloat16)


def outline_kernel(
    x_hbm, eig_hbm, mv_hbm, mr_hbm, mc_hbm, own_ref, head_y, tail_y, head_x, tail_x, low, high, means, rows_ref, sems
):
    fields, nx, ny, modes = x_hbm.shape
    copies = [
        pltpu.make_async_copy(x_hbm.at[:, :, 0:strip], low, sems.at[0]),
        pltpu.make_async_copy(x_hbm.at[:, :, ny - strip : ny], high, sems.at[1]),
        pltpu.make_async_copy(x_hbm.at[:, 0], head_x, sems.at[2]),
        pltpu.make_async_copy(x_hbm.at[:, nx - 1], tail_x, sems.at[3]),
        pltpu.make_async_copy(mv_hbm, means.at[0], sems.at[4]),
        pltpu.make_async_copy(mr_hbm, means.at[1], sems.at[5]),
        pltpu.make_async_copy(mc_hbm, means.at[2], sems.at[6]),
    ]
    copies.append(pltpu.make_async_copy(eig_hbm, rows_ref, sems.at[7]))
    for copy in [copies[7]] + copies[:7]:
        copy.start()
    copies[7].wait()
    for t in range(own_ref.shape[0]):
        own_ref[t] = rows_ref[...]
    rows = lax.broadcasted_iota(jnp.int32, (nx, nx * strip), 0)
    cells = lax.broadcasted_iota(jnp.int32, (nx, nx * strip), 1)
    places = lax.broadcasted_iota(jnp.int32, (nx, modes), 1)
    for at, held, source, edge in ((0, low, head_y, 0), (1, high, tail_y, strip - 1)):
        chosen = jnp.where(cells == rows * strip + edge, 1.0, 0.0).astype(jnp.bfloat16)
        copies[at].wait()
        for f in range(fields):
            picked = jnp.dot(
                chosen, held[f].reshape(nx * strip, modes), preferred_element_type=jnp.float32
            )
            source[f] = picked.astype(jnp.bfloat16)
    for copy in copies[4:7]:
        copy.wait()
    v, rho, stiff = (means[j, :, 0:1] for j in range(3))
    packed = jnp.zeros((nx, modes), jnp.float32)
    for j, value in enumerate((v * -0.5, rho * -0.5, -0.5 / rho, stiff * -0.5)):
        for p, part in enumerate(split(value)):
            packed = jnp.where(places == 3 * j + p, part.astype(jnp.float32), packed)
    head_y[fields] = packed.astype(jnp.bfloat16)
    for copy in copies[2:4]:
        copy.wait()


def outline(snapshots, eig_rows, tiles_n, mean_v, mean_rho, sound):
    fields, nx, ny, modes = snapshots.shape
    narrow = jnp.bfloat16
    in_hbm = [pltpu.with_memory_space_constraint(a, pltpu.HBM) for a in (snapshots, eig_rows, mean_v, mean_rho, sound)]
    hbm, vmem = pl.BlockSpec(memory_space=pltpu.HBM), pl.BlockSpec(memory_space=pltpu.VMEM)
    return pl.pallas_call(
        outline_kernel,
        out_shape=(
            jax.ShapeDtypeStruct((tiles_n,) + eig_rows.shape, narrow),
            jax.ShapeDtypeStruct((fields + 1, nx, modes), narrow),
            jax.ShapeDtypeStruct((fields, nx, modes), narrow),
            jax.ShapeDtypeStruct((fields, ny, modes), narrow),
            jax.ShapeDtypeStruct((fields, ny, modes), narrow),
        ),
        in_specs=[hbm] * 5,
        out_specs=(vmem,) * 5,
        scratch_shapes=[
            pltpu.VMEM((fields, nx, strip, modes), narrow),
            pltpu.VMEM((fields, nx, strip, modes), narrow),
            pltpu.VMEM((3, nx, ny), jnp.float32),
            pltpu.VMEM(eig_rows.shape, narrow),
            pltpu.SemaphoreType.DMA((8,)),
        ],
        compiler_params=pltpu.CompilerParams(vmem_limit_bytes=8 << 20),
        name="outline",
    )(*in_hbm)


def contract(left, right):
    return lax.dot_general(left, right, (((0,), (0,)), ((), ())), preferred_element_type=jnp.float32)


def finish_kernel(
    scale, gathered, order, g_ref, raw, ct_ref, head_x, tail_x, from_west, from_east, tail_y, from_north, vt_ref, out_ref, placed, image
):
    modes = g_ref.shape[0]
    ny = head_x.shape[1]
    nx = tail_y.shape[1]
    total = g_ref[...]

    def side(own, other, column, along, sign):
        half_c, half_rho, half_inverse, half_sound = (sign * c for c in column)
        spread_c = viscosity + half_c
        images = [
            half_c * other(0) + half_rho * other(along),
            spread_c * other(1),
            spread_c * other(2),
            spread_c * other(3),
            half_c * other(4) + half_sound * other(along),
        ]
        images[along] = images[along] + half_inverse * other(4)
        size = own.shape[1]
        for f in range(5):
            image[f * size : (f + 1) * size] = images[f].astype(jnp.bfloat16)
        return contract(own[0:5].reshape(5 * size, modes), image[0 : 5 * size])

    def plane(ref):
        return lambda f: ref[f].astype(jnp.float32)

    def column_x(i):
        return tuple(ct_ref[0:ny, j * nx + i : j * nx + i + 1] for j in (0, 2, 4, 5))

    total += side(head_x, plane(from_west), column_x(0), 1, -1.0)
    total += side(tail_x, plane(from_east), column_x(nx - 1), 1, 1.0)
    own_column = tuple(raw[j * nx : (j + 1) * nx, ny - 1 : ny] for j in (1, 2, 4, 5))
    packed = from_north[5].astype(jnp.float32)
    other_column = tuple(
        packed[:, 3 * j : 3 * j + 1] + packed[:, 3 * j + 1 : 3 * j + 2] + packed[:, 3 * j + 2 : 3 * j + 3]
        for j in range(4)
    )
    total += side(tail_y, plane(from_north), own_column, 2, 1.0)
    total += side(from_north, plane(tail_y), other_column, 2, -1.0)

    rows = modes // len(order)
    for place, tile in enumerate(gathered):
        placed[tile * rows : (tile + 1) * rows] = vt_ref[place].astype(jnp.float32)
    vt = placed[...].astype(jnp.bfloat16)
    right = None
    for part in split(total)[:2]:
        one = lax.dot_general(part, vt, (((1,), (1,)), ((), ())), preferred_element_type=jnp.float32)
        right = one if right is None else right + one
    both = None
    for part in split(right)[:2]:
        one = jnp.dot(vt, part, preferred_element_type=jnp.float32)
        both = one if both is None else both + one
    for place, tile in enumerate(order):
        out_ref[place] = (both[tile * rows : (tile + 1) * rows] * scale).astype(jnp.bfloat16)


def finish(scale, gathered, order, *operands):
    modes = operands[-1].shape[-1]
    return pl.pallas_call(
        functools.partial(finish_kernel, scale, gathered, order),
        out_shape=jax.ShapeDtypeStruct((len(order), modes // len(order), modes), jnp.bfloat16),
        in_specs=[pl.BlockSpec(memory_space=pltpu.VMEM)] * len(operands),
        out_specs=pl.BlockSpec(memory_space=pltpu.VMEM),
        scratch_shapes=[
            pltpu.VMEM((modes, modes), jnp.float32),
            pltpu.VMEM((480, modes), jnp.bfloat16),
        ],
        compiler_params=pltpu.CompilerParams(vmem_limit_bytes=12 << 20),
        name="finish",
    )(*operands)


def body(snapshots, eig_columns, mean_u, mean_v, mean_rho, mean_shear, sound):
    sections = lax.axis_size("sec")
    tiles_n = lax.axis_size("tile")
    fields, nx, ny, modes = snapshots.shape
    rows = modes // tiles_n
    scale = float(fields * nx * ny * sections * tiles_n) ** (-0.5)

    far = 4
    near = tiles_n // far
    wide = near // 2
    gathered = [
        ((x + wide // 2) % wide * far + (z + far // 2) % far) * 2 + core
        for x in range(wide)
        for z in range(far)
        for core in range(2)
    ]
    arrived = [(s + sections - 2) % sections for s in range(sections)]
    own, head_y, tail_y, head_x, tail_x = outline(
        snapshots, eig_columns.T, tiles_n, mean_v, mean_rho, sound
    )
    vt = lax.all_to_all(own, "tile", 0, 0, tiled=True, axis_index_groups=[gathered])
    from_north = lax.ppermute(head_y, "tile", [(i + 1, i) for i in range(tiles_n - 1)])
    from_west = lax.ppermute(tail_x, "sec", [(i, i + 1) for i in range(sections - 1)])
    from_east = lax.ppermute(head_x, "sec", [(i + 1, i) for i in range(sections - 1)])

    gram, raw, columns = interior(snapshots, mean_u, mean_v, mean_rho, mean_shear, sound)
    local = finish(
        scale, gathered, gathered, gram, raw, columns, head_x, tail_x, from_west, from_east, tail_y, from_north, vt
    )
    shares = lax.all_to_all(local, "tile", 0, 0, tiled=True, axis_index_groups=[gathered])
    term = shares.astype(jnp.float32).sum(0)
    terms = lax.all_to_all(
        jnp.broadcast_to(term[None], (sections, rows, modes)), "sec", 0, 0, tiled=True, axis_index_groups=[arrived]
    )
    upstream = jnp.array(arrived) <= lax.axis_index("sec")
    return jnp.where(upstream[:, None, None], terms, 0.0).sum(0)[None]


def solution(mesh):
    in_specs = (
        P(None, "sec", "tile", None),
        P(None, "tile"),
        P("sec", "tile"),
        P("sec", "tile"),
        P("sec", "tile"),
        P("sec", "tile"),
        P("sec", "tile"),
    )
    out_specs = P("sec", "tile", None)
    return jax.shard_map(body, mesh=mesh, in_specs=in_specs, out_specs=out_specs, check_vma=False)
```

time: 89.4 us -> 80.6 us (0.902)
  the two profiles are of different devices: /device:TPU:8 before, /device:TPU:1 now
where the time goes in v4:
time: 80.6 us; the launch traced here: 80.2 us
  starting transfers between devices  42.7 us (53%)
  blocking collectives  20.6 us (26%)
  Pallas kernels  12.1 us (15%)
  waiting for transfers between devices  3.21 us (4%)
    all_to_all x1, starting transfers between devices, body(): lax.all_to_all(own, 'tile', 0, 0, tiled=True, axis_index_groups=[gathered])  22 us
    all_to_all x1, blocking collectives, body(): lax.all_to_all(local, 'tile', 0, 0, tiled=True, axis_index_groups=[gather...  20.6 us
    all_to_all x1, starting transfers between devices, body(): lax.all_to_all(jnp.broadcast_to(term[None], (sections, rows, modes)), 'se...  9.33 us
    pallas_call x1, Pallas kernels, interior(): pl.pallas_call(interior_kernel, out_shape=(jax.ShapeDtypeStruct((modes, m...  8.62 us
    ppermute x1, starting transfers between devices, body(): lax.ppermute(head_y, 'tile', [(i + 1, i) for i in range(tiles_n - 1)])  6.02 us
    ppermute x1, starting transfers between devices, body(): lax.ppermute(tail_x, 'sec', [(i, i + 1) for i in range(sections - 1)])  4.03 us
    all_to_all x1, waiting for transfers between devices, body(): lax.all_to_all(jnp.broadcast_to(term[None], (sections, rows, modes)), 'se...  3.2 us
    pallas_call x1, Pallas kernels, outline(): pl.pallas_call(outline_kernel, out_shape=(jax.ShapeDtypeStruct((tiles_n,)...  2.36 us
  transfers between devices with their start and end apart: 5, of which 1 were waited for; matrix products, arithmetic and copies ran while one was open for 0% of the time, Pallas kernels for 11%

profile of v4, /device:TPU:1, one launch (start us, length us, event | category | flops | bytes accessed | tf_op | source)
XLA Modules:
  0.0 80.2 jit_solution(17068755859065342015)
XLA Ops:
  0.0 2.4 %outline.1 = (bf16[32,8,256]{2,1,0:T(8,128)(2,1)}, bf16[6,16,256]{2,1,0:T(8,128)(2,1)S(1)}, bf16[5,16,256]{2,1,0:T(8,128)(2,1)S(1)}, bf16[5,96,256]{2,1,0:T(8,128)(2,1)S(1)}, bf16[5,96,256]{2,1,0:T(8,128)(2,1)S(1)}) custom-call(bf16[5,16,96,256]{3,2,1,0:T(8,128)(2,1)} %x_hbm.3, bf16[8,256]{1,0:T(8,128)(2,1)} %bitcast.2, f32[16,96]{1,0:T(8,128)} %mv_hbm.3, ...), custom_call_target="tpu_custom_call" | custom-call | tf_op jit(solution)/shard_map/outline/pallas_call | solution.py:221
  2.4 4.0 %collective-permute-start = (bf16[5,96,256]{2,1,0:T(8,128)(2,1)S(1)}, bf16[5,96,256]{2,1,0:T(8,128)(2,1)S(1)}, u32[]{:S(2)}, u32[]{:S(2)}) collective-permute-start(bf16[5,96,256]{2,1,0:T(8,128)(2,1)S(1)} %get-tuple-element.17.tail_x), channel_id=1, source_target_pairs={{0,32},{32,64},{64,96},{96,128},{128,160},{160,192},{192,224},{224... | collective-permute-start | bytes 737288 | tf_op jit(solution)/shard_map/ppermute | solution.py:343
  6.4 1.3 %collective-permute-start.1 = (bf16[5,96,256]{2,1,0:T(8,128)(2,1)S(1)}, bf16[5,96,256]{2,1,0:T(8,128)(2,1)S(1)}, u32[]{:S(2)}, u32[]{:S(2)}) collective-permute-start(bf16[5,96,256]{2,1,0:T(8,128)(2,1)S(1)} %get-tuple-element.16.head_x), channel_id=1, source_target_pairs={{32,0},{64,32},{96,64},{128,96},{160,128},{192,160},{224,192},{256... | collective-permute-start | bytes 737288 | tf_op jit(solution)/shard_map/ppermute | solution.py:344
  7.7 6.0 %collective-permute-start.2 = (bf16[6,16,256]{2,1,0:T(8,128)(2,1)S(1)}, bf16[6,16,256]{2,1,0:T(8,128)(2,1)S(1)}, u32[]{:S(2)}, u32[]{:S(2)}) collective-permute-start(bf16[6,16,256]{2,1,0:T(8,128)(2,1)S(1)} %get-tuple-element.19), channel_id=1, source_target_pairs={{1,0},{2,1},{3,2},{4,3},{5,4},{6,5},{7,6},{8,7},{9,8},{10,9},{11,1... | collective-permute-start | bytes 147464 | tf_op jit(solution)/shard_map/ppermute | solution.py:342
  13.7 22.0 %all-to-all-start = ((bf16[32,8,256]{2,1,0:T(8,128)(2,1)}), bf16[32,8,256]{2,1,0:T(8,128)(2,1)S(1)}, u32[]{:S(2)}, u32[]{:S(2)}) async-start(bf16[32,8,256]{2,1,0:T(8,128)(2,1)} %get-tuple-element.20), calls=%async_computation | async-start | bytes 262144 | tf_op jit(solution)/shard_map/all_to_all | solution.py:341
  35.7 0.0 copy-start
  35.8 8.6 %interior.1 = (f32[256,256]{1,0:T(8,128)S(1)}, f32[128,128]{1,0:T(8,128)S(1)}, f32[128,128]{1,0:T(8,128)S(1)}) custom-call(bf16[5,16,96,256]{3,2,1,0:T(8,128)(2,1)} %x_hbm.3, f32[16,96]{1,0:T(8,128)} %mu_hbm.1, f32[16,96]{1,0:T(8,128)} %mv_hbm.3, f32[16,96]{1,0:T(8,128)} %mr_hbm.3, f32[16,96]{1,0:T(8,128)} %ms_hbm.1, f32[16,96]{1,0:T(8,128)} %mc_hbm.3), custom_call_target="tpu_custom_call" | custom-call | flops 20000000000 | bytes 10000000 | tf_op jit(solution)/shard_map/interior/pallas_call | solution.py:144
  44.4 0.0 collective-permute-done.2.from_north
  44.4 0.0 collective-permute-done.from_west
  44.4 0.0 collective-permute-done.1.from_east
  44.4 0.0 all-to-all-done.vt_ref
  44.4 1.2 %finish.1 = bf16[32,8,256]{2,1,0:T(8,128)(2,1)S(1)} custom-call(f32[256,256]{1,0:T(8,128)S(1)} %get-tuple-element.13.g_ref, f32[128,128]{1,0:T(8,128)S(1)} %get-tuple-element.14.raw, f32[128,128]{1,0:T(8,128)S(1)} %get-tuple-element.15.ct_ref, bf16[5,96,256]{2,1,0:T(8,128)(2,1)S(1)} %get-tuple-element.16.head_x, ...), custom_call_target="tpu_custom_call" | custom-call | tf_op jit(solution)/shard_map/finish/pallas_call | solution.py:307
  45.6 20.6 %all_to_all.15 = bf16[32,8,256]{2,1,0:T(8,128)(2,1)S(1)} all-to-all(bf16[32,8,256]{2,1,0:T(8,128)(2,1)S(1)} %finish.1), channel_id=1, replica_groups={{20,21,22,23,16,17,18,19,28,29,30,31,24,25,26,27,4,5,6,7,0,1,2,3,12,13,..., dimensions={0} | all-to-all | bytes 262144 | tf_op jit(solution)/shard_map/all_to_all | solution.py:350
  66.3 0.7 broadcast_in_dim.23
  66.9 9.3 %all-to-all-start.2 = ((f32[16,8,256]{2,1,0:T(8,128)}), f32[16,8,256]{2,1,0:T(8,128)S(1)}, u32[]{:S(2)}, u32[]{:S(2)}) async-start(f32[16,8,256]{2,1,0:T(8,128)} %broadcast_in_dim.23), calls=%async_computation.2 | async-start | bytes 262144 | tf_op jit(solution)/shard_map/all_to_all | solution.py:352
  76.3 0.0 copy-done
  76.3 3.2 %all-to-all-done.2 = f32[16,8,256]{2,1,0:T(8,128)S(1)} async-done(((f32[16,8,256]{2,1,0:T(8,128)}), f32[16,8,256]{2,1,0:T(8,128)S(1)}, u32[]{:S(2)}, u32[]{:S(2)}) %all-to-all-start.2) | async-done | bytes 131104 | tf_op jit(solution)/shard_map/all_to_all | solution.py:352
  79.5 0.7 select_reduce_fusion
  (2 shorter events, 0.0 us)
Async XLA Ops:
  2.4 42.0 %collective-permute-start = (bf16[5,96,256]{2,1,0:T(8,128)(2,1)S(1)}, bf16[5,96,256]{2,1,0:T(8,128)(2,1)S(1)}, u32[]{:S(2)}, u32[]{:S(2)}) collective-permute-start(bf16[5,96,256]{2,1,0:T(8,128)(2,1)S(1)} %get-tuple-element.17.tail_x), channel_id=1, source_target_pairs={{0,32},{32,64},{64,96},{96,128},{128,160},{160,192},{192,224},{224... | collective-permute-start | bytes 737288 | tf_op jit(solution)/shard_map/ppermute | solution.py:343
  6.4 38.0 %collective-permute-start.1 = (bf16[5,96,256]{2,1,0:T(8,128)(2,1)S(1)}, bf16[5,96,256]{2,1,0:T(8,128)(2,1)S(1)}, u32[]{:S(2)}, u32[]{:S(2)}) collective-permute-start(bf16[5,96,256]{2,1,0:T(8,128)(2,1)S(1)} %get-tuple-element.16.head_x), channel_id=1, source_target_pairs={{32,0},{64,32},{96,64},{128,96},{160,128},{192,160},{224,192},{256... | collective-permute-start | bytes 737288 | tf_op jit(solution)/shard_map/ppermute | solution.py:344
  7.7 36.7 %collective-permute-start.2 = (bf16[6,16,256]{2,1,0:T(8,128)(2,1)S(1)}, bf16[6,16,256]{2,1,0:T(8,128)(2,1)S(1)}, u32[]{:S(2)}, u32[]{:S(2)}) collective-permute-start(bf16[6,16,256]{2,1,0:T(8,128)(2,1)S(1)} %get-tuple-element.19), channel_id=1, source_target_pairs={{1,0},{2,1},{3,2},{4,3},{5,4},{6,5},{7,6},{8,7},{9,8},{10,9},{11,1... | collective-permute-start | bytes 147464 | tf_op jit(solution)/shard_map/ppermute | solution.py:342
  13.7 30.7 %all-to-all-start = ((bf16[32,8,256]{2,1,0:T(8,128)(2,1)}), bf16[32,8,256]{2,1,0:T(8,128)(2,1)S(1)}, u32[]{:S(2)}, u32[]{:S(2)}) async-start(bf16[32,8,256]{2,1,0:T(8,128)(2,1)} %get-tuple-element.20), calls=%async_computation | async-start | bytes 262144 | tf_op jit(solution)/shard_map/all_to_all | solution.py:341
  35.7 40.5 %copy-start = (s32[16]{0:T(128)S(1)}, s32[16]{0:T(128)}, u32[]{:S(2)}) copy-start(s32[16]{0:T(128)} %constant.10.clone) | copy-start | bytes 196
  66.9 12.6 %all-to-all-start.2 = ((f32[16,8,256]{2,1,0:T(8,128)}), f32[16,8,256]{2,1,0:T(8,128)S(1)}, u32[]{:S(2)}, u32[]{:S(2)}) async-start(f32[16,8,256]{2,1,0:T(8,128)} %broadcast_in_dim.23), calls=%async_computation.2 | async-start | bytes 262144 | tf_op jit(solution)/shard_map/all_to_all | solution.py:352

commit v5 on v4

--- a/solution.py
+++ b/solution.py
@@ -12,10 +12,11 @@
 pad = 8
 strip = 16
 lanes = 128
+period = 4
 
 
 def interior_kernel(
-    x_hbm, mu_hbm, mv_hbm, mr_hbm, ms_hbm, mc_hbm, g_ref, raw, ct_ref, xb, qf, means, even, odd, sems
+    x_hbm, mu_hbm, mv_hbm, mr_hbm, ms_hbm, mc_hbm, g_ref, raw, ct_ref, xb, q0, q1, q2, q3, means, i0, i1, sems
 ):
     fields, nx, ny, modes = x_hbm.shape
     halves = modes // lanes
@@ -32,9 +33,18 @@
     for i in range(nx):
         copy(i).start()
 
+    ring, image_ring = (q0, q1, q2, q3), (i0, i1)
+    edge = jnp.zeros((pad, lanes), jnp.float32)
     raw[...] = jnp.zeros_like(raw)
-    qf[0] = jnp.zeros(qf.shape[1:], jnp.float32)
-    odd[...] = jnp.zeros_like(odd)
+    for plane in ring:
+        for f in range(fields):
+            for h in range(halves):
+                plane[f, h, 0:pad] = edge
+                plane[f, h, pad + ny : 2 * pad + ny] = edge
+    q3[...] = jnp.zeros_like(q3)
+    i1[...] = jnp.zeros_like(i1)
+    xb[nx] = jnp.zeros(xb.shape[1:], xb.dtype)
+    xb[nx + 1] = jnp.zeros(xb.shape[1:], xb.dtype)
     g_ref[...] = jnp.zeros_like(g_ref)
     for one in coefficients:
         one.wait()
@@ -43,19 +53,16 @@
         raw[j * nx : (j + 1) * nx, 0:ny] = value
     ct_ref[...] = raw[...].T
 
-    def widen(i):
-        edge = jnp.zeros((pad, lanes), jnp.float32)
+    def widen(i, plane):
         for f in range(fields):
             for h in range(halves):
                 part = slice(h * lanes, (h + 1) * lanes)
-                qf[i + 1, f, h, 0:pad] = edge
-                qf[i + 1, f, h, pad + ny : 2 * pad + ny] = edge
                 for y in range(0, ny, strip):
-                    qf[i + 1, f, h, pad + y : pad + y + strip] = xb[i, f, y : y + strip, part].astype(
+                    plane[f, h, pad + y : pad + y + strip] = xb[i, f, y : y + strip, part].astype(
                         jnp.float32
                     )
 
-    def apply(i, image):
+    def apply(i, behind, middle, ahead, image):
         zero = jnp.minimum(i, 0)
         turned = pltpu.roll(ct_ref[...], 128 - i, 1)
         for y in range(0, ny, strip):
@@ -69,19 +76,19 @@
             for h in range(halves):
 
                 def east(f):
-                    return qf[i + 2, f, h, top : top + strip]
+                    return ahead[f, h, top : top + strip]
 
                 def west(f):
-                    return qf[i, f, h, top : top + strip]
+                    return behind[f, h, top : top + strip]
 
                 def north(f):
-                    return qf[i + 1, f, h, pl.ds(zero + top + 1, strip)]
+                    return middle[f, h, pl.ds(zero + top + 1, strip)]
 
                 def south(f):
-                    return qf[i + 1, f, h, pl.ds(zero + top - 1, strip)]
+                    return middle[f, h, pl.ds(zero + top - 1, strip)]
 
                 def here(f):
-                    return qf[i + 1, f, h, top : top + strip]
+                    return middle[f, h, top : top + strip]
 
                 def flow(f):
                     return half_u * (east(f) - west(f)) + half_v * (north(f) - south(f))
@@ -112,31 +119,29 @@
             preferred_element_type=jnp.float32,
         )
 
-    copy(0).wait()
-    widen(0)
+    for i in range(2):
+        copy(i).wait()
+        widen(i, ring[i])
 
     def step(p, carry):
-        i = 2 * p
-        copy(i + 1).wait()
-        widen(i + 1)
-        apply(i, even)
-        gather(jnp.maximum(i - 1, 0), odd)
-
-        @pl.when(i + 2 < nx)
+        first = period * p
+        for one in range(2, period):
+            copy(first + one).wait()
+
+        @pl.when(first + period < nx)
         def _():
-            copy(i + 2).wait()
-            widen(i + 2)
-
-        @pl.when(i + 2 == nx)
-        def _():
-            qf[nx + 1] = jnp.zeros(qf.shape[1:], jnp.float32)
-
-        apply(i + 1, odd)
-        gather(i, even)
+            copy(first + period).wait()
+            copy(first + period + 1).wait()
+
+        for one in range(period):
+            i = first + one
+            apply(i, ring[(one - 1) % 4], ring[one], ring[(one + 1) % 4], image_ring[one % 2])
+            gather(jnp.maximum(i - 1, 0), image_ring[(one + 1) % 2])
+            widen(i + 2, ring[(one + 2) % 4])
         return carry
 
-    lax.fori_loop(0, nx // 2, step, 0)
-    gather(nx - 1, odd)
+    lax.fori_loop(0, nx // period, step, 0)
+    gather(nx - 1, image_ring[(nx - 1) % 2])
 
 
 def interior(snapshots, *means):
@@ -151,8 +156,11 @@
         in_specs=[pl.BlockSpec(memory_space=pltpu.HBM)] * 6,
         out_specs=(pl.BlockSpec(memory_space=pltpu.VMEM),) * 3,
         scratch_shapes=[
-            pltpu.VMEM((nx, fields, ny, modes), jnp.bfloat16),
-            pltpu.VMEM((nx + 2, fields, modes // lanes, ny + 2 * pad, lanes), jnp.float32),
+            pltpu.VMEM((nx + 2, fields, ny, modes), jnp.bfloat16),
+            pltpu.VMEM((fields, modes // lanes, ny + 2 * pad, lanes), jnp.float32),
+            pltpu.VMEM((fields, modes // lanes, ny + 2 * pad, lanes), jnp.float32),
+            pltpu.VMEM((fields, modes // lanes, ny + 2 * pad, lanes), jnp.float32),
+            pltpu.VMEM((fields, modes // lanes, ny + 2 * pad, lanes), jnp.float32),
             pltpu.VMEM((5, nx, ny), jnp.float32),
             pltpu.VMEM((fields * ny, modes), jnp.bfloat16),
             pltpu.VMEM((fields * ny, modes), jnp.bfloat16),
@@ -329,6 +337,12 @@
     near = tiles_n // far
     wide = near // 2
     gathered = [
+        ((x + 2) % wide * far + (z + 3) % far) * 2 + core
+        for x in range(wide)
+        for z in range(far)
+        for core in range(2)
+    ]
+    summed = [
         ((x + wide // 2) % wide * far + (z + far // 2) % far) * 2 + core
         for x in range(wide)
         for z in range(far)
@@ -345,9 +359,9 @@
 
     gram, raw, columns = interior(snapshots, mean_u, mean_v, mean_rho, mean_shear, sound)
     local = finish(
-        scale, gathered, gathered, gram, raw, columns, head_x, tail_x, from_west, from_east, tail_y, from_north, vt
-    )
-    shares = lax.all_to_all(local, "tile", 0, 0, tiled=True, axis_index_groups=[gathered])
+        scale, gathered, summed, gram, raw, columns, head_x, tail_x, from_west, from_east, tail_y, from_north, vt
+    )
+    shares = lax.all_to_all(local, "tile", 0, 0, tiled=True, axis_index_groups=[summed])
     term = shares.astype(jnp.float32).sum(0)
     terms = lax.all_to_all(
         jnp.broadcast_to(term[None], (sections, rows, modes)), "sec", 0, 0, tiled=True, axis_index_groups=[arrived]

time: 80.6 us -> 79.3 us (0.984)
  starting transfers between devices: 42.7 us -> 38 us
  blocking collectives: 20.6 us -> 23.9 us
    all_to_all x1, starting transfers between devices: 22 us -> 17.2 us  [body(): lax.all_to_all(own, 'tile', 0, 0, tiled=True, axis_index_groups=[gathered])]
    all_to_all x1, blocking collectives: 20.6 us -> 23.9 us  [body(): lax.all_to_all(local, 'tile', 0, 0, tiled=True, axis_index_groups=[summed])]
  transfers between devices with their start and end apart: 5 -> 5, of which waited for: 1 -> 1; matrix products, arithmetic and copies ran while one was open for 0% -> 0% of each run, Pallas kernels for 11% -> 10%
where the time goes in v5:
time: 79.3 us; the launch traced here: 78.9 us
  starting transfers between devices  38 us (48%)
  blocking collectives  23.9 us (30%)
  Pallas kernels  11.6 us (15%)
  waiting for transfers between devices  3.98 us (5%)
    all_to_all x1, blocking collectives, body(): lax.all_to_all(local, 'tile', 0, 0, tiled=True, axis_index_groups=[summed])  23.9 us
    all_to_all x1, starting transfers between devices, body(): lax.all_to_all(own, 'tile', 0, 0, tiled=True, axis_index_groups=[gathered])  17.2 us
    all_to_all x1, starting transfers between devices, body(): lax.all_to_all(jnp.broadcast_to(term[None], (sections, rows, modes)), 'se...  9.48 us
    pallas_call x1, Pallas kernels, interior(): pl.pallas_call(interior_kernel, out_shape=(jax.ShapeDtypeStruct((modes, m...  8.05 us
    ppermute x1, starting transfers between devices, body(): lax.ppermute(head_y, 'tile', [(i + 1, i) for i in range(tiles_n - 1)])  6.02 us
    ppermute x1, starting transfers between devices, body(): lax.ppermute(tail_x, 'sec', [(i, i + 1) for i in range(sections - 1)])  4.03 us
    all_to_all x1, waiting for transfers between devices, body(): lax.all_to_all(jnp.broadcast_to(term[None], (sections, rows, modes)), 'se...  3.97 us
    pallas_call x1, Pallas kernels, outline(): pl.pallas_call(outline_kernel, out_shape=(jax.ShapeDtypeStruct((tiles_n,)...  2.36 us
  transfers between devices with their start and end apart: 5, of which 1 were waited for; matrix products, arithmetic and copies ran while one was open for 0% of the time, Pallas kernels for 10%

profile of v5, /device:TPU:1, one launch (start us, length us, event | category | flops | bytes accessed | tf_op | source)
XLA Modules:
  0.0 78.9 jit_solution(16064361480845026452)
XLA Ops:
  0.0 2.4 %outline.1 = (bf16[32,8,256]{2,1,0:T(8,128)(2,1)}, bf16[6,16,256]{2,1,0:T(8,128)(2,1)S(1)}, bf16[5,16,256]{2,1,0:T(8,128)(2,1)S(1)}, bf16[5,96,256]{2,1,0:T(8,128)(2,1)S(1)}, bf16[5,96,256]{2,1,0:T(8,128)(2,1)S(1)}) custom-call(bf16[5,16,96,256]{3,2,1,0:T(8,128)(2,1)} %x_hbm.3, bf16[8,256]{1,0:T(8,128)(2,1)} %bitcast.2, f32[16,96]{1,0:T(8,128)} %mv_hbm.3, ...), custom_call_target="tpu_custom_call" | custom-call | tf_op jit(solution)/shard_map/outline/pallas_call | solution.py:229
  2.4 4.0 %collective-permute-start = (bf16[5,96,256]{2,1,0:T(8,128)(2,1)S(1)}, bf16[5,96,256]{2,1,0:T(8,128)(2,1)S(1)}, u32[]{:S(2)}, u32[]{:S(2)}) collective-permute-start(bf16[5,96,256]{2,1,0:T(8,128)(2,1)S(1)} %get-tuple-element.17.tail_x), channel_id=1, source_target_pairs={{0,32},{32,64},{64,96},{96,128},{128,160},{160,192},{192,224},{224... | collective-permute-start | bytes 737288 | tf_op jit(solution)/shard_map/ppermute | solution.py:357
  6.4 1.3 %collective-permute-start.1 = (bf16[5,96,256]{2,1,0:T(8,128)(2,1)S(1)}, bf16[5,96,256]{2,1,0:T(8,128)(2,1)S(1)}, u32[]{:S(2)}, u32[]{:S(2)}) collective-permute-start(bf16[5,96,256]{2,1,0:T(8,128)(2,1)S(1)} %get-tuple-element.16.head_x), channel_id=1, source_target_pairs={{32,0},{64,32},{96,64},{128,96},{160,128},{192,160},{224,192},{256... | collective-permute-start | bytes 737288 | tf_op jit(solution)/shard_map/ppermute | solution.py:358
  7.7 6.0 %collective-permute-start.2 = (bf16[6,16,256]{2,1,0:T(8,128)(2,1)S(1)}, bf16[6,16,256]{2,1,0:T(8,128)(2,1)S(1)}, u32[]{:S(2)}, u32[]{:S(2)}) collective-permute-start(bf16[6,16,256]{2,1,0:T(8,128)(2,1)S(1)} %get-tuple-element.19), channel_id=1, source_target_pairs={{1,0},{2,1},{3,2},{4,3},{5,4},{6,5},{7,6},{8,7},{9,8},{10,9},{11,1... | collective-permute-start | bytes 147464 | tf_op jit(solution)/shard_map/ppermute | solution.py:356
  13.7 17.2 %all-to-all-start = ((bf16[32,8,256]{2,1,0:T(8,128)(2,1)}), bf16[32,8,256]{2,1,0:T(8,128)(2,1)S(1)}, u32[]{:S(2)}, u32[]{:S(2)}) async-start(bf16[32,8,256]{2,1,0:T(8,128)(2,1)} %get-tuple-element.20), calls=%async_computation | async-start | bytes 262144 | tf_op jit(solution)/shard_map/all_to_all | solution.py:355
  30.9 0.0 copy-start
  30.9 8.1 %interior.1 = (f32[256,256]{1,0:T(8,128)S(1)}, f32[128,128]{1,0:T(8,128)S(1)}, f32[128,128]{1,0:T(8,128)S(1)}) custom-call(bf16[5,16,96,256]{3,2,1,0:T(8,128)(2,1)} %x_hbm.3, f32[16,96]{1,0:T(8,128)} %mu_hbm.1, f32[16,96]{1,0:T(8,128)} %mv_hbm.3, f32[16,96]{1,0:T(8,128)} %mr_hbm.3, f32[16,96]{1,0:T(8,128)} %ms_hbm.1, f32[16,96]{1,0:T(8,128)} %mc_hbm.3), custom_call_target="tpu_custom_call" | custom-call | flops 20000000000 | bytes 10000000 | tf_op jit(solution)/shard_map/interior/pallas_call | solution.py:149
  39.0 0.0 collective-permute-done.2.from_north
  39.0 0.0 collective-permute-done.from_west
  39.0 0.0 collective-permute-done.1.from_east
  39.0 0.0 all-to-all-done.vt_ref
  39.0 1.2 %finish.1 = bf16[32,8,256]{2,1,0:T(8,128)(2,1)S(1)} custom-call(f32[256,256]{1,0:T(8,128)S(1)} %get-tuple-element.13.g_ref, f32[128,128]{1,0:T(8,128)S(1)} %get-tuple-element.14.raw, f32[128,128]{1,0:T(8,128)S(1)} %get-tuple-element.15.ct_ref, bf16[5,96,256]{2,1,0:T(8,128)(2,1)S(1)} %get-tuple-element.16.head_x, ...), custom_call_target="tpu_custom_call" | custom-call | tf_op jit(solution)/shard_map/finish/pallas_call | solution.py:315
  40.2 23.9 %all_to_all.15 = bf16[32,8,256]{2,1,0:T(8,128)(2,1)S(1)} all-to-all(bf16[32,8,256]{2,1,0:T(8,128)(2,1)S(1)} %finish.1), channel_id=1, replica_groups={{20,21,22,23,16,17,18,19,28,29,30,31,24,25,26,27,4,5,6,7,0,1,2,3,12,13,..., dimensions={0} | all-to-all | bytes 262144 | tf_op jit(solution)/shard_map/all_to_all | solution.py:364
  64.1 0.7 broadcast_in_dim.23
  64.8 9.5 %all-to-all-start.2 = ((f32[16,8,256]{2,1,0:T(8,128)}), f32[16,8,256]{2,1,0:T(8,128)S(1)}, u32[]{:S(2)}, u32[]{:S(2)}) async-start(f32[16,8,256]{2,1,0:T(8,128)} %broadcast_in_dim.23), calls=%async_computation.2 | async-start | bytes 262144 | tf_op jit(solution)/shard_map/all_to_all | solution.py:366
  74.3 0.0 copy-done
  74.3 4.0 %all-to-all-done.2 = f32[16,8,256]{2,1,0:T(8,128)S(1)} async-done(((f32[16,8,256]{2,1,0:T(8,128)}), f32[16,8,256]{2,1,0:T(8,128)S(1)}, u32[]{:S(2)}, u32[]{:S(2)}) %all-to-all-start.2) | async-done | bytes 131104 | tf_op jit(solution)/shard_map/all_to_all | solution.py:366
  78.3 0.7 select_reduce_fusion
  (2 shorter events, 0.0 us)
Async XLA Ops:
  2.4 36.6 %collective-permute-start = (bf16[5,96,256]{2,1,0:T(8,128)(2,1)S(1)}, bf16[5,96,256]{2,1,0:T(8,128)(2,1)S(1)}, u32[]{:S(2)}, u32[]{:S(2)}) collective-permute-start(bf16[5,96,256]{2,1,0:T(8,128)(2,1)S(1)} %get-tuple-element.17.tail_x), channel_id=1, source_target_pairs={{0,32},{32,64},{64,96},{96,128},{128,160},{160,192},{192,224},{224... | collective-permute-start | bytes 737288 | tf_op jit(solution)/shard_map/ppermute | solution.py:357
  6.4 32.6 %collective-permute-start.1 = (bf16[5,96,256]{2,1,0:T(8,128)(2,1)S(1)}, bf16[5,96,256]{2,1,0:T(8,128)(2,1)S(1)}, u32[]{:S(2)}, u32[]{:S(2)}) collective-permute-start(bf16[5,96,256]{2,1,0:T(8,128)(2,1)S(1)} %get-tuple-element.16.head_x), channel_id=1, source_target_pairs={{32,0},{64,32},{96,64},{128,96},{160,128},{192,160},{224,192},{256... | collective-permute-start | bytes 737288 | tf_op jit(solution)/shard_map/ppermute | solution.py:358
  7.7 31.3 %collective-permute-start.2 = (bf16[6,16,256]{2,1,0:T(8,128)(2,1)S(1)}, bf16[6,16,256]{2,1,0:T(8,128)(2,1)S(1)}, u32[]{:S(2)}, u32[]{:S(2)}) collective-permute-start(bf16[6,16,256]{2,1,0:T(8,128)(2,1)S(1)} %get-tuple-element.19), channel_id=1, source_target_pairs={{1,0},{2,1},{3,2},{4,3},{5,4},{6,5},{7,6},{8,7},{9,8},{10,9},{11,1... | collective-permute-start | bytes 147464 | tf_op jit(solution)/shard_map/ppermute | solution.py:356
  13.7 25.3 %all-to-all-start = ((bf16[32,8,256]{2,1,0:T(8,128)(2,1)}), bf16[32,8,256]{2,1,0:T(8,128)(2,1)S(1)}, u32[]{:S(2)}, u32[]{:S(2)}) async-start(bf16[32,8,256]{2,1,0:T(8,128)(2,1)} %get-tuple-element.20), calls=%async_computation | async-start | bytes 262144 | tf_op jit(solution)/shard_map/all_to_all | solution.py:355
  30.9 43.3 %copy-start = (s32[16]{0:T(128)S(1)}, s32[16]{0:T(128)}, u32[]{:S(2)}) copy-start(s32[16]{0:T(128)} %constant.10.clone) | copy-start | bytes 196
  64.8 13.5 %all-to-all-start.2 = ((f32[16,8,256]{2,1,0:T(8,128)}), f32[16,8,256]{2,1,0:T(8,128)S(1)}, u32[]{:S(2)}, u32[]{:S(2)}) async-start(f32[16,8,256]{2,1,0:T(8,128)} %broadcast_in_dim.23), calls=%async_computation.2 | async-start | bytes 262144 | tf_op jit(solution)/shard_map/all_to_all | solution.py:366
